TPU v7x, 128 devices: a whole 4x4x4 slice. The times are simulated.
128 devices in a mesh: rep: 4 (over x_hi, core), own: 32 (over x_lo, z, y).
Axes of the slice: x: 4 (x_hi: 2, x_lo: 2; x = x_hi * 2 + x_lo), y: 4, z: 4, core: 2. Of those that a mesh axis runs over, the one named last changes fastest.
Arguments:
- replica_delta: float32 [4, 32, 256, 1792], P('rep', None, 'own'), may hold values from -6 to 6
- layer_basis: float32 [4, 1792, 64], replicated, may hold values from -0.25 to 0.25
- layer_of: int32 [32], replicated, may hold values from 0 to 3
- owner_of: int32 [32], replicated, may hold values from 0 to 31, as said below
- weights_owned: float32 [64, 256, 1792], P('own'), may hold values from -6 to 6
- momentum_owned: float32 [64, 256, 1792], P('own'), may hold values from -4 to 4
Outputs:
- new_weights: float32 [64, 256, 1792], P('own')
- new_momentum: float32 [64, 256, 1792], P('own')
- replica_weights: float32 [32, 256, 1792], P(None, 'own')
Inputs may be any that keep to these rules, and one draw needn't show every extreme that they name: `owner_of`: no owner holds more than 2 blocks, and some owner holds exactly 2; the slots of an owner are taken in the order of the blocks.
All inputs are finite; a program needn't handle non-finite values.
Results may differ from a plain program's by a relative error of at most 0.00007.
Values sent between devices are 32-bit elements; how exact they have to be, the bound alone decides.
A program may use at most 128 MiB of HBM per device.

v0:
```python
import jax
import jax.numpy as jnp
from jax import lax
from jax.sharding import PartitionSpec as P

momentum_decay = 0.9
outer_rate = 0.7


def slot_table(owner_of, capacity):
    blocks = owner_of.shape[0]
    same_owner = owner_of[None, :] == owner_of[:, None]
    positions = jnp.arange(blocks, dtype=jnp.int32)
    earlier = positions[None, :] < positions[:, None]
    rank_in = jnp.sum((same_owner & earlier).astype(jnp.int32), axis=1)
    return owner_of * capacity + rank_in


def local(replica_delta, layer_basis, layer_of, owner_of, weights_owned, momentum_owned):
    highest = lax.Precision.HIGHEST
    own_count = lax.axis_size("own")
    rep_count = lax.axis_size("rep")
    capacity = weights_owned.shape[0]
    slot_of = slot_table(owner_of, capacity)
    slot_total = capacity * own_count
    holding = (slot_of[None, :] == jnp.arange(slot_total, dtype=jnp.int32)[:, None]).astype(
        jnp.float32
    )
    chosen = jnp.take(layer_basis, layer_of, axis=0)
    coeffs = jnp.einsum("bnd,bdk->bnk", replica_delta[0], chosen, precision=highest)
    averaged = lax.psum(coeffs, "rep") / rep_count
    outer_grad = jnp.einsum("bnk,bdk->bnd", averaged, chosen, precision=highest)
    weights_rows, momentum_rows = (
        lax.all_to_all(weights_owned, "own", split_axis=1, concat_axis=0, tiled=True),
        lax.all_to_all(momentum_owned, "own", split_axis=1, concat_axis=0, tiled=True),
    )
    weights_rows = jnp.take(weights_rows, slot_of, axis=0)
    momentum_rows = jnp.take(momentum_rows, slot_of, axis=0)
    momentum_next = momentum_decay * momentum_rows + outer_grad
    replica_weights = weights_rows - outer_rate * (outer_grad + momentum_decay * momentum_next)
    placed_weights = jnp.einsum("sb,bnd->snd", holding, replica_weights, precision=highest)
    placed_momentum = jnp.einsum("sb,bnd->snd", holding, momentum_next, precision=highest)
    new_weights, new_momentum = (
        lax.all_to_all(placed_weights, "own", split_axis=0, concat_axis=1, tiled=True),
        lax.all_to_all(placed_momentum, "own", split_axis=0, concat_axis=1, tiled=True),
    )
    return (new_weights, new_momentum, replica_weights)


def solution(mesh):
    placed = (
        P("rep", None, "own", None),
        P(),
        P(),
        P(),
        P("own", None, None),
        P("own", None, None),
    )
    return jax.shard_map(
        local,
        mesh=mesh,
        in_specs=placed,
        out_specs=(P("own", None, None), P("own", None, None), P(None, "own", None)),
        check_vma=False,
    )
```

profile of v0, /device:TPU:1, one launch (start us, length us, event | category | flops | bytes accessed | tf_op | source)
XLA Modules:
  0.0 282.2 jit_solution(16814883334786525864)
XLA Ops:
  7.2 0.0 copy-start
  7.2 6.8 %copy.35 = f32[2,256,1792]{2,0,1:T(2,128)} copy(f32[2,256,1792]{2,1,0:T(8,128)} %param.12) | data formatting | bytes 7340032 | tf_op args[4]
  14.0 9.9 %all-to-all-start = ((f32[2,256,1792]{2,0,1:T(2,128)}), f32[2,256,1792]{2,0,1:T(2,128)}, u32[]{:S(2)}, u32[]{:S(2)}) async-start(f32[2,256,1792]{2,0,1:T(2,128)} %copy.35), calls=%async_computation | async-start | bytes 7340032 | tf_op jit(solution)/shard_map/all_to_all | solution.py:34
  24.0 6.7 %copy.38 = f32[2,256,1792]{2,0,1:T(2,128)} copy(f32[2,256,1792]{2,1,0:T(8,128)} %param.13) | data formatting | bytes 7340032 | tf_op args[5]
  30.7 0.0 copy-start.4
  30.7 39.8 %all-to-all-done = f32[2,256,1792]{2,0,1:T(2,128)} async-done(((f32[2,256,1792]{2,0,1:T(2,128)}), f32[2,256,1792]{2,0,1:T(2,128)}, u32[]{:S(2)}, u32[]{:S(2)}) %all-to-all-start) | async-done | bytes 3670048 | tf_op jit(solution)/shard_map/all_to_all | solution.py:34
  70.5 8.5 %all-to-all-start.1 = ((f32[2,256,1792]{2,0,1:T(2,128)}), f32[2,256,1792]{2,0,1:T(2,128)}, u32[]{:S(2)}, u32[]{:S(2)}) async-start(f32[2,256,1792]{2,0,1:T(2,128)} %copy.38), calls=%async_computation.1 | async-start | bytes 7340032 | tf_op jit(solution)/shard_map/all_to_all | solution.py:35
  79.0 0.2 all-reduce.2.cloned.1.call-start
  79.2 0.0 copy-done.4
  79.2 0.0 copy-done
  79.2 6.7 %gather_fusion = f32[32,1792,64]{1,2,0:T(8,128)} fusion(f32[4,1792,64]{1,2,0:T(8,128)S(1)} %copy-done, s32[1024]{0:T(1024)S(1)} %pad_clamp_fusion), kind=kCustom, calls=%fused_computation.2 | custom fusion | bytes 29360256 | tf_op jit(solution)/shard_map/jit(_take)/gather | solution.py:29
  85.9 0.0 copy-start.3
  85.9 17.0 %fusion.14 = f32[32,8,64]{2,1,0:T(8,128)} fusion(f32[1,32,8,1792]{3,2,1,0:T(8,128)} %param.8, f32[32,1792,64]{1,2,0:T(8,128)} %gather_fusion, pred[32]{0:T(512)(128)(4,1)S(1)} %compare_and_fusion.1), kind=kOutput, calls=%fused_computation.23 | convolution fusion | flops 355991552 | bytes 16580640 | tf_op jit(solution)/shard_map/bnd,bdk->bnk/dot_general | solution.py:30
  103.0 0.0 all-reduce.2.cloned.1.call-update
  103.0 0.0 copy-done.3
  103.0 0.2 convert_reduce_fusion
  103.2 2.3 copy.58
  105.5 2.3 copy.37
  107.8 18.8 %all-to-all-done.1 = f32[2,256,1792]{2,0,1:T(2,128)} async-done(((f32[2,256,1792]{2,0,1:T(2,128)}), f32[2,256,1792]{2,0,1:T(2,128)}, u32[]{:S(2)}, u32[]{:S(2)}) %all-to-all-start.1) | async-done | bytes 3670048 | tf_op jit(solution)/shard_map/all_to_all | solution.py:35
  126.6 2.3 copy.57
  128.9 2.3 copy.40
  131.2 4.0 %gather_fusion.1 = f32[32,8,1792]{2,1,0:T(8,128)} fusion(f32[64,8,1792]{2,1,0:T(8,128)} %bitcast.37, s32[1024]{0:T(1024)S(1)} %pad_clamp_fusion.1), kind=kCustom, calls=%fused_computation.clone | custom fusion | bytes 3670144 | tf_op jit(solution)/shard_map/jit(_take)/gather | solution.py:37
  135.1 3.9 %gather_fusion.2 = f32[32,8,1792]{2,1,0:T(8,128)} fusion(f32[64,8,1792]{2,1,0:T(8,128)} %bitcast.38, s32[1024]{0:T(1024)S(1)} %pad_clamp_fusion.1), kind=kCustom, calls=%fused_computation.1.clone | custom fusion | bytes 3670144 | tf_op jit(solution)/shard_map/jit(_take)/gather | solution.py:38
  139.1 6.6 %all-reduce.2.cloned.1.call-done = f32[32,8,64]{2,1,0:T(8,128)} async-done(((f32[32,8,64]{2,1,0:T(8,128)}), f32[32,8,64]{2,1,0:T(8,128)}) %all-reduce.2.cloned.1.call-update) | async-done | bytes 65552 | tf_op jit(solution)/shard_map/psum | solution.py:31
  145.7 11.4 %fusion.13 = (f32[32,8,1792]{2,1,0:T(8,128)S(1)}, f32[32,8,1792]{2,1,0:T(8,128)S(1)}) fusion(f32[32,8,1792]{2,1,0:T(8,128)} %gather_fusion.2, pred[32]{0:T(512)(128)(4,1)S(1)} %get-tuple-element.4, f32[32,8,1792]{2,1,0:T(8,128)} %gather_fusion.1, f32[32,1792,64]{1,2,0:T(8,128)} %gather_fusion, pred[32]{0:T(512)(128)(4,1)S(1)} %compare_and_fusion.1, ...), kind=kOutput, calls=%fused_computation.21 | convolution fusion | flops 359677952 | bytes 22085696 | tf_op jit(solution)/shard_map/bnk,bdk->bnd/dot_general | solution.py:32
  157.1 0.0 copy-start.2
  157.1 2.3 fusion.9
  159.4 4.0 %copy.45 = f32[64,8,1792]{2,1,0:T(8,128)} copy(f32[64,8,1792]{2,0,1:T(8,128)S(1)} %fusion.9) | data formatting | bytes 7340032 | tf_op jit(solution)/shard_map/sb,bnd->snd/dot_general | solution.py:42
  163.4 7.1 %all-to-all-start.3 = ((f32[64,8,1792]{2,1,0:T(8,128)}), f32[64,8,1792]{2,1,0:T(8,128)}, u32[]{:S(2)}, u32[]{:S(2)}) async-start(f32[64,8,1792]{2,1,0:T(8,128)} %copy.45), calls=%async_computation.3 | async-start | bytes 7340032 | tf_op jit(solution)/shard_map/all_to_all | solution.py:45
  170.5 0.0 copy-done.2
  170.5 2.3 fusion.11
  172.8 4.0 %copy.42 = f32[64,8,1792]{2,1,0:T(8,128)} copy(f32[64,8,1792]{2,0,1:T(8,128)S(1)} %fusion.11) | data formatting | bytes 7340032 | tf_op jit(solution)/shard_map/sb,bnd->snd/dot_general | solution.py:41
  176.7 41.7 %all-to-all-done.3 = f32[64,8,1792]{2,1,0:T(8,128)} async-done(((f32[64,8,1792]{2,1,0:T(8,128)}), f32[64,8,1792]{2,1,0:T(8,128)}, u32[]{:S(2)}, u32[]{:S(2)}) %all-to-all-start.3) | async-done | bytes 3670048 | tf_op jit(solution)/shard_map/all_to_all | solution.py:45
  218.4 6.5 %all-to-all-start.2 = ((f32[64,8,1792]{2,1,0:T(8,128)}), f32[64,8,1792]{2,1,0:T(8,128)}, u32[]{:S(2)}, u32[]{:S(2)}) async-start(f32[64,8,1792]{2,1,0:T(8,128)} %copy.42), calls=%async_computation.2 | async-start | bytes 7340032 | tf_op jit(solution)/shard_map/all_to_all | solution.py:44
  224.9 4.1 %copy.55 = f32[2,32,8,1792]{3,2,1,0:T(8,128)} copy(f32[2,32,8,1792]{3,2,0,1:T(8,128)} %bitcast.13) | data formatting | bytes 7340032 | tf_op jit(solution)/shard_map/all_to_all | solution.py:45
  229.1 42.0 %all-to-all-done.2 = f32[64,8,1792]{2,1,0:T(8,128)} async-done(((f32[64,8,1792]{2,1,0:T(8,128)}), f32[64,8,1792]{2,1,0:T(8,128)}, u32[]{:S(2)}, u32[]{:S(2)}) %all-to-all-start.2) | async-done | bytes 3670048 | tf_op jit(solution)/shard_map/all_to_all | solution.py:44
  271.0 0.0 copy-start.1
  271.0 4.3 %copy.56 = f32[2,32,8,1792]{3,2,1,0:T(8,128)} copy(f32[2,32,8,1792]{3,2,0,1:T(8,128)} %bitcast.10) | data formatting | bytes 7340032 | tf_op jit(solution)/shard_map/all_to_all | solution.py:44
  275.3 0.0 copy-done.1
  (6 shorter events, 0.0 us)
Async XLA Ops:
  7.2 72.1 %copy-start = (f32[4,1792,64]{1,2,0:T(8,128)S(1)}, f32[4,1792,64]{1,2,0:T(8,128)}, u32[]{:S(2)}) copy-start(f32[4,1792,64]{1,2,0:T(8,128)} %param.9) | copy-start | bytes 5505028
  14.0 56.5 %all-to-all-start = ((f32[2,256,1792]{2,0,1:T(2,128)}), f32[2,256,1792]{2,0,1:T(2,128)}, u32[]{:S(2)}, u32[]{:S(2)}) async-start(f32[2,256,1792]{2,0,1:T(2,128)} %copy.35), calls=%async_computation | async-start | bytes 7340032 | tf_op jit(solution)/shard_map/all_to_all | solution.py:34
  30.7 48.5 %copy-start.4 = (s32[32]{0:T(128)S(1)}, s32[32]{0:T(128)}, u32[]{:S(2)}) copy-start(s32[32]{0:T(128)} %param.10) | copy-start | bytes 388
  70.5 56.1 %all-to-all-start.1 = ((f32[2,256,1792]{2,0,1:T(2,128)}), f32[2,256,1792]{2,0,1:T(2,128)}, u32[]{:S(2)}, u32[]{:S(2)}) async-start(f32[2,256,1792]{2,0,1:T(2,128)} %copy.38), calls=%async_computation.1 | async-start | bytes 7340032 | tf_op jit(solution)/shard_map/all_to_all | solution.py:35
  79.0 66.7 %all-reduce.2.cloned.1.call-start = ((), (), s32[]{:S(2)}) async-start(), calls=%async_computation.4 | async-start | bytes 262144 | tf_op jit(solution)/shard_map/psum | solution.py:31
  85.9 17.1 %copy-start.3 = (s32[32]{0:T(128)S(1)}, s32[32]{0:T(128)}, u32[]{:S(2)}) copy-start(s32[32]{0:T(128)} %param.11) | copy-start | bytes 388
  157.1 13.4 %copy-start.2 = (f32[32,8,1792]{2,1,0:T(8,128)}, f32[32,8,1792]{2,1,0:T(8,128)S(1)}, u32[]{:S(2)}) copy-start(f32[32,8,1792]{2,1,0:T(8,128)S(1)} %get-tuple-element.7) | copy-start | bytes 5505028
  163.4 55.1 %all-to-all-start.3 = ((f32[64,8,1792]{2,1,0:T(8,128)}), f32[64,8,1792]{2,1,0:T(8,128)}, u32[]{:S(2)}, u32[]{:S(2)}) async-start(f32[64,8,1792]{2,1,0:T(8,128)} %copy.45), calls=%async_computation.3 | async-start | bytes 7340032 | tf_op jit(solution)/shard_map/all_to_all | solution.py:45
  218.4 52.6 %all-to-all-start.2 = ((f32[64,8,1792]{2,1,0:T(8,128)}), f32[64,8,1792]{2,1,0:T(8,128)}, u32[]{:S(2)}, u32[]{:S(2)}) async-start(f32[64,8,1792]{2,1,0:T(8,128)} %copy.42), calls=%async_computation.2 | async-start | bytes 7340032 | tf_op jit(solution)/shard_map/all_to_all | solution.py:44
  271.0 4.3 %copy-start.1 = (f32[4,1792,64]{1,2,0:T(8,128)S(1)}, f32[4,1792,64]{1,2,0:T(8,128)}, u32[]{:S(2)}) copy-start(f32[4,1792,64]{1,2,0:T(8,128)} %param.9) | copy-start | bytes 5505028
Sparse Core Ops, SparseCore 0:
  103.1 42.5 all-reduce.1
where the time goes:
time: 284 us; the launch traced here: 282 us
  waiting for transfers between devices  149 us (52%)
  local copies, waits for them, and re-layouts  53.6 us (19%)
  matrix products  33 us (12%)
  starting transfers between devices  32.2 us (11%)
  between operations  14.2 us (5%)
    all_to_all x1, waiting for transfers between devices, local(): lax.all_to_all(placed_weights, 'own', split_axis=0, concat_axis=1, tiled=...  42 us
    all_to_all x1, waiting for transfers between devices, local(): lax.all_to_all(placed_momentum, 'own', split_axis=0, concat_axis=1, tiled...  41.7 us
    all_to_all x1, waiting for transfers between devices, local(): lax.all_to_all(weights_owned, 'own', split_axis=1, concat_axis=0, tiled=T...  39.8 us
    all_to_all x1, waiting for transfers between devices, local(): lax.all_to_all(momentum_owned, 'own', split_axis=1, concat_axis=0, tiled=...  18.8 us
    dot_general x1, matrix products, local(): jnp.einsum('bnd,bdk->bnk', replica_delta[0], chosen, precision=highest)  17 us
    unnamed x12, local copies, waits for them, and re-layouts  13.6 us
    dot_general x1, matrix products, local(): outer_grad = jnp.einsum('bnk,bdk->bnd', averaged, chosen, precision=highest)  11.4 us
    all_to_all x1, starting transfers between devices, local(): lax.all_to_all(weights_owned, 'own', split_axis=1, concat_axis=0, tiled=T...  9.93 us
  transfers between devices with their start and end apart: 5, of which 5 were waited for; matrix products, arithmetic and copies ran while one was open for 21% of the time, Pallas kernels for 0%

commit v1 on v0

v1 whole, which is shorter than its diff:
```python
import functools

import jax
import jax.numpy as jnp
from jax import lax
from jax.experimental import pallas as pl
from jax.experimental.pallas import tpu as pltpu
from jax.sharding import PartitionSpec as P

momentum_decay = 0.9
outer_rate = 0.7

MESH = pl.DeviceIdType.MESH
HIGHEST = lax.Precision.HIGHEST
D = 1792
HALF = D // 2
RANK = 64
BLOCKS = 32
OWN = 32
TILE = 256

FAR = [(1, 2), (3, 2), (2, 1), (2, 3), (1, 1), (3, 3), (1, 3), (3, 1), (2, 2),
       (2, 0), (0, 2), (1, 0), (0, 1), (3, 0), (0, 3)]


def place():
    rep = lax.axis_index("rep")
    own = lax.axis_index("own")
    x = (rep // 2) * 2 + own // 16
    return x, own % 4, (own // 4) % 4, rep % 2


def device(x, y, z, core):
    return ((x // 2) * 2 + core, (x % 2) * 16 + z * 4 + y)


def send(src, dst, send_sem, recv_sem, to):
    return pltpu.make_async_remote_copy(
        src_ref=src, dst_ref=dst, send_sem=send_sem, recv_sem=recv_sem,
        device_id=to, device_id_type=MESH,
    )


def kernel(
    owner_s, owner_v, layer_v, delta_hbm, basis_hbm, weights_hbm, momentum_hbm,
    new_weights, new_momentum, replica,
    w, m, d, bt, q, r, relay, og, part, part_sum, from_core, from_x, packed, placed,
    slots,
    load_sem, near_send, near_recv, far_send, far_recv, relay_send, relay_recv,
    side_send, side_recv, swap_send, swap_recv, packed_send, packed_recv, own_sem,
):
    x, y, z, core = place()
    lo, hi = x % 2, x // 2
    me = lo * 16 + z * 4 + y
    other = 1 - core
    x_up, x_down, x_far = (x + 1) % 4, (x + 3) % 4, (x + 2) % 4
    up, down = device(x_up, y, z, core), device(x_down, y, z, core)
    partner, opposite = device(x, y, z, other), device(x_far, y, z, core)

    mine = pl.ds(pl.multiple_of(core * HALF, 128), HALF)
    rest = pl.ds(pl.multiple_of(other * HALF, 128), HALF)
    loads = [
        (weights_hbm.at[:, :, :, mine], w.at[:, :, :, mine]),
        (momentum_hbm.at[:, :, :, mine], m.at[:, :, :, mine]),
        (delta_hbm, d),
        (basis_hbm, bt),
        (weights_hbm.at[:, :, :, rest], w.at[:, :, :, rest]),
        (momentum_hbm.at[:, :, :, rest], m.at[:, :, :, rest]),
    ]
    copies = [pltpu.make_async_copy(a, b, load_sem.at[i]) for i, (a, b) in enumerate(loads)]
    for copy in copies:
        copy.start()

    barrier = pltpu.get_barrier_semaphore()
    count = 0
    for dy, dz in FAR:
        for side in range(2):
            to = device((1 - side) * x + side * (hi * 2 + 1 - lo), (y + dy) % 4, (z + dz) % 4, core)
            pl.semaphore_signal(barrier, inc=1, device_id=to, device_id_type=MESH)
            count += 1
    for to in (up, down, partner, opposite):
        pl.semaphore_signal(barrier, inc=1, device_id=to, device_id_type=MESH)
        count += 1

    def slot_body(b, carry):
        owner = owner_s[b]
        rank = lax.fori_loop(
            0, BLOCKS, lambda e, t: t + jnp.where((owner_s[e] == owner) & (e < b), 1, 0), 0
        )
        slots[b] = owner * 2 + rank
        return carry

    copies[0].wait()
    copies[1].wait()

    def q_body(o, carry):
        for half in range(2):
            @pl.when(core == half)
            def _():
                cols = slice(half * HALF, (half + 1) * HALF)
                for s in range(2):
                    q[o, s] = w[s, o, :, cols] - (outer_rate * momentum_decay * momentum_decay) * m[s, o, :, cols]
        return carry

    lax.fori_loop(0, OWN, q_body, 0)
    lax.fori_loop(0, BLOCKS, slot_body, 0)

    pl.semaphore_wait(barrier, count)

    def far_copies(i):
        dy, dz = FAR[i]
        ty, tz = (y + dy) % 4, (z + dz) % 4
        to = device(x, ty, tz, core)
        direct = send(q.at[lo * 16 + tz * 4 + ty], r.at[core, me], far_send, far_recv.at[i], to)
        onward = send(
            q.at[(1 - lo) * 16 + tz * 4 + ty, hi], relay.at[z * 4 + y], relay_send, relay_recv.at[i], to
        )
        return direct, onward

    own_copy = pltpu.make_async_copy(q.at[me], r.at[core, me], own_sem.at[0])
    own_copy.start()
    own_swap = send(q.at[me], r.at[core, me], swap_send, swap_recv.at[15], partner)
    own_swap.start()
    across = (1 - lo) * 16 + z * 4 + y
    side = [
        send(q.at[across, hi], r.at[core, me, hi], side_send, side_recv.at[0, 15], up),
        send(q.at[across, hi], r.at[core, me, hi], side_send, side_recv.at[1, 15], down),
    ]
    for copy in side:
        copy.start()
    far = [far_copies(i) for i in range(15)]
    first = 8
    for direct, onward in far[:first]:
        onward.start()
        direct.start()

    row = lax.broadcasted_iota(jnp.int32, (256, 1), 0)
    lane256 = lax.broadcasted_iota(jnp.int32, (1, 256), 1)
    lane128 = lax.broadcasted_iota(jnp.int32, (1, 128), 1)
    lane32 = lax.broadcasted_iota(jnp.int32, (1, BLOCKS), 1)
    layer_row = layer_v[...]
    owner_row = owner_v[...]
    layer_col = jnp.sum(jnp.where(row // 8 == lane32, layer_row, 0), axis=1, keepdims=True)
    in_layer = (lane256 // RANK) == layer_col
    low = lane128 < RANK

    copies[2].wait()
    copies[3].wait()
    every = lax.dot_general(
        d[...], bt[...], (((1,), (1,)), ((), ())), precision=HIGHEST,
        preferred_element_type=jnp.float32,
    )
    every = jnp.where(in_layer, every, 0.0)
    both = every[:, :128] + every[:, 128:]
    both = both + pltpu.roll(both, RANK, 1)
    part[...] = jnp.where(low, both[:128], both[128:])
    core_copy = send(part, from_core, packed_send.at[0], packed_recv.at[0], partner)
    core_copy.start()

    blk_col = lax.broadcasted_iota(jnp.int32, (BLOCKS, 1), 0)
    owner_col = jnp.sum(jnp.where(blk_col == lane32, owner_row, 0), axis=1, keepdims=True)
    rank_col = jnp.sum(
        jnp.where((owner_col == owner_row) & (lane32 < blk_col), 1, 0), axis=1, keepdims=True
    )
    slot_col = owner_col * 2 + rank_col
    layer_blk = jnp.sum(jnp.where(blk_col == lane32, layer_row, 0), axis=1, keepdims=True)
    slot_lane = jnp.sum(jnp.where(lane256 // 8 == blk_col, slot_col, 0), axis=0, keepdims=True)
    same_row = (row % 8) == (lane256 % 8)
    pick = [
        jnp.where(((row // 8) * 2 + j == slot_lane) & same_row, 1.0, 0.0) for j in range(2)
    ]
    used, layers = [], []
    for j in range(2):
        hit = slot_col == me * 2 + j
        used.append(jnp.sum(jnp.where(hit, 1.0, 0.0), axis=0, keepdims=True))
        layers.append(jnp.sum(jnp.where(hit, layer_blk, 0), axis=0, keepdims=True))

    core_copy.wait()
    part_sum[...] = part[...] + from_core[...]
    x_copy = send(part_sum, from_x, packed_send.at[1], packed_recv.at[1], opposite)
    x_copy.start()
    x_copy.wait()
    averaged = (part_sum[...] + from_x[...]) * 0.25
    turned = pltpu.roll(averaged, RANK, 1)
    dup = jnp.concatenate(
        [jnp.where(low, averaged, turned), jnp.where(low, turned, averaged)], axis=0
    )
    chosen = [
        jnp.dot(p, dup, precision=HIGHEST, preferred_element_type=jnp.float32) for p in pick
    ]
    packed[...] = jnp.where(low, chosen[0], chosen[1]).reshape(OWN, 8, 128)

    def spread(pairs, keep):
        return jnp.where(keep, jnp.concatenate([pairs, pairs], axis=1), 0.0)

    og_coeffs = spread(dup, in_layer)

    own_packed = pltpu.make_async_copy(packed.at[me], placed.at[me], own_sem.at[1])
    own_packed.start()
    for dy, dz in [(0, 0)] + FAR:
        for s in range(2):
            if s == 0 and (dy, dz) == (0, 0):
                continue
            ty, tz = (y + dy) % 4, (z + dz) % 4
            to_lo = lo if s == 0 else 1 - lo
            send(
                packed.at[to_lo * 16 + tz * 4 + ty], placed.at[me], packed_send.at[2],
                packed_recv.at[2], device(hi * 2 + to_lo, ty, tz, core),
            ).start()
    for direct, onward in far[first:]:
        onward.start()
        direct.start()

    def og_body(j, carry):
        cols = pl.ds(pl.multiple_of(j * TILE, TILE), TILE)
        og[:, cols] = jnp.dot(
            og_coeffs, bt[:, cols], precision=HIGHEST, preferred_element_type=jnp.float32
        )
        return carry

    lax.fori_loop(0, D // TILE, og_body, 0)

    def onward_step(i):
        dy, dz = FAR[i]
        fy, fz = (y + 4 - dy) % 4, (z + 4 - dz) % 4
        src = lo * 16 + fz * 4 + fy
        far[i][1].wait_recv()
        for k, to in enumerate((up, down)):
            send(relay.at[fz * 4 + fy], r.at[core, src, hi], side_send, side_recv.at[k, i], to).start()

    def swap_step(i):
        dy, dz = FAR[i]
        fy, fz = (y + 4 - dy) % 4, (z + 4 - dz) % 4
        src = lo * 16 + fz * 4 + fy
        far[i][0].wait_recv()
        send(r.at[core, src], r.at[core, src], swap_send, swap_recv.at[i], partner).start()

    def side_step(i):
        dy, dz = FAR[i] if i < 15 else (0, 0)
        fy, fz = (y + 4 - dy) % 4, (z + 4 - dz) % 4
        src = (1 - lo) * 16 + fz * 4 + fy
        hi_down, hi_up = x_down // 2, x_up // 2
        send(relay.at[0], r.at[core, src, hi_down], side_send, side_recv.at[0, i], up).wait_recv()
        send(relay.at[0], r.at[core, src, hi_up], side_send, side_recv.at[1, i], down).wait_recv()
        send(r.at[core, src], r.at[core, src], swap_send, swap_recv.at[16 + i], partner).start()

    for i in range(first):
        onward_step(i)
        swap_step(i)

    own_packed.wait()
    send(packed.at[pl.ds(0, 31)], placed.at[pl.ds(0, 31)], packed_send.at[2], packed_recv.at[2], up).wait_recv()
    copies[4].wait()
    copies[5].wait()
    got = placed[...].reshape(256, 128)
    got_turned = pltpu.roll(got, RANK, 1)
    for j in range(2):
        pairs = jnp.where(low, got, got_turned) if j == 0 else jnp.where(low, got_turned, got)
        coeffs = spread(pairs, jnp.broadcast_to((lane256 // RANK) == layers[j], (256, 256)))
        use = used[j]

        def owner_body(t, carry, j=j, coeffs=coeffs, use=use):
            cols = pl.ds(pl.multiple_of(t * TILE, TILE), TILE)
            grad = jnp.dot(
                coeffs, bt[:, cols], precision=HIGHEST, preferred_element_type=jnp.float32
            ) * use
            grad = grad.reshape(OWN, 8, TILE)
            moved = (momentum_decay * m[j, :, :, cols] + grad) * use
            new_momentum[j, :, :, cols] = moved
            new_weights[j, :, :, cols] = (
                w[j, :, :, cols] - outer_rate * (grad + momentum_decay * moved)
            ) * use
            return carry

        lax.fori_loop(0, D // TILE, owner_body, 0)

    for i in range(first, 15):
        onward_step(i)
        swap_step(i)
    side_step(15)
    for i in range(15):
        side_step(i)

    own_copy.wait()
    for i in range(32):
        send(r.at[0, 0], r.at[other, 0], swap_send, swap_recv.at[i], partner).wait_recv()

    def out_body(b, carry):
        slot = slots[b]
        for half in range(2):
            cols = slice(half * HALF, (half + 1) * HALF)
            replica[b, :, cols] = r[half, slot // 2, slot % 2] - (
                outer_rate * (1.0 + momentum_decay)
            ) * og[pl.ds(pl.multiple_of(b * 8, 8), 8), cols]
        return carry

    lax.fori_loop(0, BLOCKS, out_body, 0)

    send(q.at[pl.ds(0, 15)], q.at[pl.ds(0, 15)], far_send, far_recv.at[0], up).wait_send()
    send(relay.at[pl.ds(0, 15)], relay.at[pl.ds(0, 15)], relay_send, far_recv.at[0], up).wait_send()
    send(q.at[pl.ds(0, 16)], q.at[pl.ds(0, 16)], side_send, far_recv.at[0], up).wait_send()
    send(q, q, swap_send, far_recv.at[0], up).wait_send()
    send(packed.at[pl.ds(0, 31)], placed.at[pl.ds(0, 31)], packed_send.at[2], packed_recv.at[2], up).wait_send()


def local(replica_delta, layer_basis, layer_of, owner_of, weights_owned, momentum_owned):
    vmem = pl.BlockSpec(memory_space=pltpu.VMEM)
    smem = pl.BlockSpec(memory_space=pltpu.SMEM)
    hbm = pl.BlockSpec(memory_space=pl.ANY)
    dma = pltpu.SemaphoreType.DMA
    f32 = jnp.float32
    basis = jnp.swapaxes(layer_basis, 1, 2).reshape(4 * RANK, D)
    delta = replica_delta.reshape(256, D)
    weights = weights_owned.reshape(2, OWN, 8, D)
    momentum = momentum_owned.reshape(2, OWN, 8, D)
    new_weights, new_momentum, replica = pl.pallas_call(
        kernel,
        out_shape=(
            pltpu.VMEM((2, OWN, 8, D), f32),
            pltpu.VMEM((2, OWN, 8, D), f32),
            pltpu.VMEM((BLOCKS, 8, D), f32),
        ),
        in_specs=[smem, vmem, vmem, hbm, hbm, hbm, hbm],
        out_specs=(vmem, vmem, vmem),
        scratch_shapes=[
            pltpu.VMEM((2, OWN, 8, D), f32),
            pltpu.VMEM((2, OWN, 8, D), f32),
            pltpu.VMEM((256, D), f32),
            pltpu.VMEM((256, D), f32),
            pltpu.VMEM((OWN, 2, 8, HALF), f32),
            pltpu.VMEM((2, OWN, 2, 8, HALF), f32),
            pltpu.VMEM((16, 8, HALF), f32),
            pltpu.VMEM((256, D), f32),
            pltpu.VMEM((128, 128), f32),
            pltpu.VMEM((128, 128), f32),
            pltpu.VMEM((128, 128), f32),
            pltpu.VMEM((128, 128), f32),
            pltpu.VMEM((OWN, 8, 128), f32),
            pltpu.VMEM((OWN, 8, 128), f32),
            pltpu.SMEM((BLOCKS,), jnp.int32),
            dma((6,)),
            dma, dma,
            dma, dma((15,)),
            dma, dma((15,)),
            dma, dma((2, 16)),
            dma, dma((32,)),
            dma((3,)), dma((3,)),
            dma((2,)),
        ],
        compiler_params=pltpu.CompilerParams(
            collective_id=0, has_side_effects=True, vmem_limit_bytes=48 << 20
        ),
        name="outer_step",
    )(
        owner_of, owner_of.reshape(1, BLOCKS), layer_of.reshape(1, BLOCKS),
        delta, basis, weights, momentum,
    )
    return (
        new_weights.reshape(2, 256, D),
        new_momentum.reshape(2, 256, D),
        replica,
    )


def solution(mesh):
    placed = (
        P("rep", None, "own", None),
        P(),
        P(),
        P(),
        P("own", None, None),
        P("own", None, None),
    )
    return jax.shard_map(
        local,
        mesh=mesh,
        in_specs=placed,
        out_specs=(P("own", None, None), P("own", None, None), P(None, "own", None)),
        check_vma=False,
    )
```

time: 284 us -> 55.3 us (0.19)
  waiting for transfers between devices: 149 us -> 0 us
  Pallas kernels: 0 us -> 49.6 us
  local copies, waits for them, and re-layouts: 53.6 us -> 4.9 us
  matrix products: 33 us -> 0 us
  starting transfers between devices: 32.2 us -> 0 us
  between operations: 14.2 us -> 0.64 us
    all_to_all x4 -> x0, waiting for transfers between devices: 142 us -> none  [the longest x1 42 us: local(): lax.all_to_all(placed_weights, 'own', split_axis=0, concat_axis=1, tiled=...]
    pallas_call x0 -> x1, Pallas kernels: none -> 49.6 us  [local(): pl.pallas_call(kernel, out_shape=(pltpu.VMEM((2, OWN, 8, D), f32), pltpu....]
    dot_general x4 -> x0, matrix products: 33 us -> none  [the longest x1 17 us: local(): jnp.einsum('bnd,bdk->bnk', replica_delta[0], chosen, precision=highest)]
    all_to_all x4 -> x0, starting transfers between devices: 32 us -> none  [the longest x1 9.93 us: local(): lax.all_to_all(weights_owned, 'own', split_axis=1, concat_axis=0, tiled=T...]
    all_to_all x6 -> x0, local copies, waits for them, and re-layouts: 17.5 us -> none  [the longest x2 4.56 us: local(): lax.all_to_all(weights_owned, 'own', split_axis=1, concat_axis=0, tiled=T...]
    gather x3 -> x0, local copies, waits for them, and re-layouts: 14.6 us -> none  [the longest x1 6.68 us: local(): chosen = jnp.take(layer_basis, layer_of, axis=0)]
    unnamed x12 -> x3, local copies, waits for them, and re-layouts: 13.6 us -> 4.9 us
    dot_general x2 -> x0, local copies, waits for them, and re-layouts: 7.93 us -> none  [the longest x1 3.96 us: local(): jnp.einsum('sb,bnd->snd', holding, momentum_next, precision=highest)]
  transfers between devices with their start and end apart: 5 -> 0, of which waited for: 5 -> 0; matrix products, arithmetic and copies ran while one was open for 21% -> 0% of each run, Pallas kernels for 0% -> 0%
where the time goes in v1:
time: 55.3 us; the launch traced here: 55.1 us
  Pallas kernels  49.6 us (90%)
  local copies, waits for them, and re-layouts  4.9 us (9%)
  between operations  0.64 us (1%)
    pallas_call x1, Pallas kernels, local(): pl.pallas_call(kernel, out_shape=(pltpu.VMEM((2, OWN, 8, D), f32), pltpu....  49.6 us
    unnamed x3, local copies, waits for them, and re-layouts  4.9 us

profile of v1, /device:TPU:1, one launch (start us, length us, event | category | flops | bytes accessed | tf_op | source)
XLA Modules:
  0.0 55.1 jit_solution(15192077534639324908)
XLA Ops:
  0.6 49.6 %outer_step.1 = (f32[2,32,8,1792]{3,2,1,0:T(8,128)S(1)}, f32[2,32,8,1792]{3,2,1,0:T(8,128)S(1)}, f32[32,8,1792]{2,1,0:T(8,128)S(1)}) custom-call(s32[32]{0:T(128)} %owner_s.1, s32[1,32]{1,0:T(1,128)} %bitcast.16, s32[1,32]{1,0:T(1,128)} %bitcast.17, f32[256,1792]{1,0:T(8,128)} %bitcast.14, f32[256,1792]{1,0:T(8,128)} %bitcast.15, ...), custom_call_target="tpu_custom_call" | custom-call | tf_op jit(solution)/shard_map/outer_step/pallas_call | solution.py:316
  50.2 1.8 %copy.12 = f32[2,256,1792]{2,1,0:T(8,128)} copy(f32[2,256,1792]{2,1,0:T(8,128)S(1)} %bitcast.11) | data formatting | bytes 7340032
  52.1 1.8 %copy.13 = f32[2,256,1792]{2,1,0:T(8,128)} copy(f32[2,256,1792]{2,1,0:T(8,128)S(1)} %bitcast.10) | data formatting | bytes 7340032
  53.9 1.2 %copy.14 = f32[32,8,1792]{2,1,0:T(8,128)} copy(f32[32,8,1792]{2,1,0:T(8,128)S(1)} %get-tuple-element.11) | data formatting | bytes 3670016

commit v2 on v0

v2 whole, which is shorter than its diff:
```python
import jax
import jax.numpy as jnp
from jax import lax
from jax.experimental import pallas as pl
from jax.experimental.pallas import tpu as pltpu
from jax.sharding import PartitionSpec as P

momentum_decay = 0.9
outer_rate = 0.7

MESH = pl.DeviceIdType.MESH
HIGHEST = lax.Precision.HIGHEST
D = 1792
HALF = D // 2
RANK = 64
BLOCKS = 32
OWN = 32
TILE = 256
BF16 = jnp.bfloat16
F32 = jnp.float32

DZ = [0, 1, 3, 2]
NEAR = [(1, 0), (3, 0), (2, 0)] + [(dy, dz) for dz in DZ[1:] for dy in (0, 1, 3, 2)]
FAR = [(1, 2), (3, 2), (2, 1), (2, 3), (1, 1), (3, 3), (1, 3), (3, 1), (2, 2),
       (2, 0), (0, 2), (1, 0), (0, 1), (3, 0), (0, 3)]
FIRST = 6


def place():
    rep = lax.axis_index("rep")
    own = lax.axis_index("own")
    x = (rep // 2) * 2 + own // 16
    return x, own % 4, (own // 4) % 4, rep % 2


def device(x, y, z, core):
    return ((x // 2) * 2 + core, (x % 2) * 16 + z * 4 + y)


def send(src, dst, send_sem, recv_sem, to):
    return pltpu.make_async_remote_copy(
        src_ref=src, dst_ref=dst, send_sem=send_sem, recv_sem=recv_sem,
        device_id=to, device_id_type=MESH,
    )


def split(value):
    high = value.astype(BF16)
    return high, (value - high.astype(F32)).astype(BF16)


def dot(a, b, dims=((1,), (0,))):
    return lax.dot_general(a, b, (dims, ((), ())), preferred_element_type=F32)


def exchange(
    owner_hbm, layer_hbm, delta_hbm, basis_hbm, weights_hbm, momentum_hbm,
    new_weights, new_momentum, r, og, slots,
    owner_v, layer_v, w, m, d, bt, bt_high, bt_low, q, relay, parts, packed, placed,
    load_sem, far_send, far_recv, relay_send, relay_recv, side_send, side_recv,
    swap_send, swap_recv, part_send, part_recv, packed_send, packed_recv, own_sem,
    table_sem,
):
    x, y, z, core = place()
    lo, hi = x % 2, x // 2
    rep = hi * 2 + core
    me = lo * 16 + z * 4 + y
    other = 1 - core
    x_up, x_down, x_far = (x + 1) % 4, (x + 3) % 4, (x + 2) % 4
    up, down = device(x_up, y, z, core), device(x_down, y, z, core)
    partner = device(x, y, z, other)
    peers = [partner, device(x_far, y, z, core), device(x_far, y, z, other)]

    tables = [
        pltpu.make_async_copy(a, b, table_sem.at[i])
        for i, (a, b) in enumerate(((owner_hbm, owner_v), (layer_hbm, layer_v)))
    ]
    for copy in tables:
        copy.start()

    mine = pl.ds(pl.multiple_of(core * HALF, 128), HALF)
    rest = pl.ds(pl.multiple_of(other * HALF, 128), HALF)
    loads = []
    for dz in DZ:
        tz = (z + dz) % 4
        loads.append((weights_hbm.at[:, :, tz, :, :, mine], w.at[:, :, tz, :, :, mine]))
        loads.append((momentum_hbm.at[:, :, tz, :, :, mine], m.at[:, :, tz, :, :, mine]))
    loads += [
        (basis_hbm, bt),
        (delta_hbm, d),
        (weights_hbm.at[:, :, :, :, :, rest], w.at[:, :, :, :, :, rest]),
        (momentum_hbm.at[:, :, :, :, :, rest], m.at[:, :, :, :, :, rest]),
    ]
    copies = [pltpu.make_async_copy(a, b, load_sem.at[i]) for i, (a, b) in enumerate(loads)]
    for copy in copies:
        copy.start()

    barrier = pltpu.get_barrier_semaphore()
    targets = [up, down] + peers
    for dy, dz in FAR:
        for tx in (x, hi * 2 + 1 - lo):
            targets.append(device(tx, (y + dy) % 4, (z + dz) % 4, core))
    for to in targets:
        pl.semaphore_signal(barrier, inc=1, device_id=to, device_id_type=MESH)

    row = lax.broadcasted_iota(jnp.int32, (256, 1), 0)
    lane256 = lax.broadcasted_iota(jnp.int32, (1, 256), 1)
    lane128 = lax.broadcasted_iota(jnp.int32, (1, 128), 1)
    lane32 = lax.broadcasted_iota(jnp.int32, (1, BLOCKS), 1)
    blk_col = lax.broadcasted_iota(jnp.int32, (BLOCKS, 1), 0)
    for copy in tables:
        copy.wait()
    layer_row = layer_v[...]
    owner_row = owner_v[...]
    layer_col = jnp.sum(jnp.where(row // 8 == lane32, layer_row, 0), axis=1, keepdims=True)
    in_layer = (lane256 // RANK) == layer_col
    low = lane128 < RANK
    owner_col = jnp.sum(jnp.where(blk_col == lane32, owner_row, 0), axis=1, keepdims=True)
    same = owner_col == owner_row
    slot_col = owner_col * 2 + jnp.sum(
        jnp.where(same & (lane32 < blk_col), 1, 0), axis=1, keepdims=True
    )
    slots[...] = jnp.sum(jnp.where(blk_col == lane128, slot_col, 0), axis=0, keepdims=True)

    def q_rows(k):
        tz = (z + DZ[k]) % 4
        copies[2 * k].wait()
        copies[2 * k + 1].wait()
        for half in range(2):
            @pl.when(core == half)
            def _():
                cols = slice(half * HALF, (half + 1) * HALF)
                for s in range(2):
                    q[:, tz, :, s] = w[s, :, tz, :, :, cols] - (
                        outer_rate * momentum_decay * momentum_decay
                    ) * m[s, :, tz, :, :, cols]

    def direct_copy(i):
        dy, dz = FAR[i]
        ty, tz = (y + dy) % 4, (z + dz) % 4
        return send(
            q.at[lo, tz, ty], r.at[core, me], far_send, far_recv.at[i], device(x, ty, tz, core)
        )

    def onward_copy(i):
        dy, dz = NEAR[i]
        ty, tz = (y + dy) % 4, (z + dz) % 4
        return send(
            q.at[1 - lo, tz, ty, hi], relay.at[z * 4 + y], relay_send, relay_recv.at[i],
            device(x, ty, tz, core),
        )

    onward = [onward_copy(i) for i in range(15)]
    direct = [direct_copy(i) for i in range(15)]
    own_copy = pltpu.make_async_copy(q.at[lo, z, y], r.at[core, me], own_sem.at[0])
    own_swap = send(q.at[lo, z, y], r.at[core, me], swap_send, swap_recv.at[15], partner)
    side = [
        send(q.at[1 - lo, z, y, hi], r.at[core, me, hi], side_send, side_recv.at[k, 15], to)
        for k, to in enumerate((up, down))
    ]

    q_rows(0)
    q_rows(1)
    pl.semaphore_wait(barrier, len(targets))
    for copy in side + onward[:3]:
        copy.start()
    q_rows(2)
    for copy in onward[3:7]:
        copy.start()
    q_rows(3)
    for copy in onward[7:11]:
        copy.start()
    own_copy.start()
    own_swap.start()

    copies[8].wait()
    for t in range(D // TILE):
        cols = slice(t * TILE, (t + 1) * TILE)
        bt_high[:, cols], bt_low[:, cols] = split(bt[:, cols])
    for copy in onward[11:] + direct[:FIRST]:
        copy.start()
    copies[9].wait()
    every = jnp.zeros((256, 256), F32)
    for t in range(D // TILE):
        cols = slice(t * TILE, (t + 1) * TILE)
        high, low_part = split(d[:, cols])
        along = ((1,), (1,))
        every = every + (
            dot(high, bt_high[:, cols], along)
            + (dot(high, bt_low[:, cols], along) + dot(low_part, bt_high[:, cols], along))
        )
    every = jnp.where(in_layer, every, 0.0)
    both = every[:, :128] + every[:, 128:]
    both = both + pltpu.roll(both, RANK, 1)
    parts[rep] = jnp.where(low, both[:128], both[128:])

    layer_blk = jnp.sum(jnp.where(blk_col == lane32, layer_row, 0), axis=1, keepdims=True)
    slot_lane = jnp.sum(jnp.where(lane256 // 8 == blk_col, slot_col, 0), axis=0, keepdims=True)
    same_row = (row % 8) == (lane256 % 8)
    pick = [
        jnp.where(((row // 8) * 2 + j == slot_lane) & same_row, 1.0, 0.0) for j in range(2)
    ]
    used, layers = [], []
    for j in range(2):
        hit = slot_col == me * 2 + j
        used.append(jnp.sum(jnp.where(hit, 1.0, 0.0), axis=0, keepdims=True))
        layers.append(jnp.sum(jnp.where(hit, layer_blk, 0), axis=0, keepdims=True))

    part_copies = [
        send(parts.at[rep], parts.at[rep], part_send.at[k], part_recv.at[k], to)
        for k, to in enumerate(peers)
    ]
    for copy in part_copies[1:] + part_copies[:1]:
        copy.start()

    def source(dy, dz):
        return (y + 4 - dy) % 4, (z + 4 - dz) % 4

    def onward_step(i):
        fy, fz = source(*NEAR[i])
        src = lo * 16 + fz * 4 + fy
        onward[i].wait_recv()
        for k, to in enumerate((up, down)):
            send(relay.at[fz * 4 + fy], r.at[core, src, hi], side_send, side_recv.at[k, i], to).start()

    def swap_step(i):
        fy, fz = source(*FAR[i])
        src = lo * 16 + fz * 4 + fy
        direct[i].wait_recv()
        send(r.at[core, src], r.at[core, src], swap_send, swap_recv.at[i], partner).start()

    def side_step(i):
        fy, fz = source(*(NEAR[i] if i < 15 else (0, 0)))
        src = (1 - lo) * 16 + fz * 4 + fy
        for k, from_x in enumerate((x_down, x_up)):
            send(
                relay.at[0], r.at[core, src, from_x // 2], side_send, side_recv.at[k, i], up
            ).wait_recv()
        send(r.at[core, src], r.at[core, src], swap_send, swap_recv.at[16 + i], partner).start()

    for i in range(9):
        onward_step(i)
    for copy in part_copies:
        copy.wait_recv()
    averaged = ((parts[0] + parts[1]) + (parts[2] + parts[3])) * 0.25
    turned = pltpu.roll(averaged, RANK, 1)
    dup = jnp.concatenate(
        [jnp.where(low, averaged, turned), jnp.where(low, turned, averaged)], axis=0
    )
    chosen = [
        jnp.dot(p, dup, precision=HIGHEST, preferred_element_type=F32) for p in pick
    ]
    packed[...] = jnp.where(low, chosen[0], chosen[1]).reshape(OWN, 8, 128)

    def spread(pairs, keep):
        return jnp.where(keep, jnp.concatenate([pairs, pairs], axis=1), 0.0)

    og_high, og_low = split(spread(dup, in_layer))

    own_packed = pltpu.make_async_copy(packed.at[me], placed.at[me], own_sem.at[1])
    own_packed.start()
    for dy, dz in FAR + [(0, 0)]:
        for s in range(2):
            if s == 0 and (dy, dz) == (0, 0):
                continue
            ty, tz = (y + dy) % 4, (z + dz) % 4
            to_lo = lo if s == 0 else 1 - lo
            send(
                packed.at[to_lo * 16 + tz * 4 + ty], placed.at[me], packed_send,
                packed_recv, device(hi * 2 + to_lo, ty, tz, core),
            ).start()
    for copy in direct[FIRST:]:
        copy.start()

    for i in range(9, 15):
        onward_step(i)

    def og_body(t, carry):
        cols = pl.ds(pl.multiple_of(t * TILE, TILE), TILE)
        high = bt_high[:, cols]
        og[:, cols] = dot(og_high, high) + (dot(og_high, bt_low[:, cols]) + dot(og_low, high))
        return carry

    lax.fori_loop(0, D // TILE, og_body, 0)
    for i in (15, *range(7)):
        side_step(i)
    for i in range(FIRST):
        swap_step(i)

    own_packed.wait()
    tiles = send(packed.at[pl.ds(0, 31)], placed.at[pl.ds(0, 31)], packed_send, packed_recv, up)
    tiles.wait_recv()
    copies[10].wait()
    copies[11].wait()
    got = placed[...].reshape(256, 128)
    got_turned = pltpu.roll(got, RANK, 1)
    for j in range(2):
        pairs = jnp.where(low, got, got_turned) if j == 0 else jnp.where(low, got_turned, got)
        in_slot = jnp.broadcast_to((lane256 // RANK) == layers[j], (256, 256))
        slot_high, slot_low = split(spread(pairs, in_slot))
        use = used[j]

        def owner_body(t, carry, j=j, slot_high=slot_high, slot_low=slot_low, use=use):
            cols = pl.ds(pl.multiple_of(t * TILE, TILE), TILE)
            high = bt_high[:, cols]
            grad = dot(slot_high, high) + (dot(slot_high, bt_low[:, cols]) + dot(slot_low, high))
            moved = (momentum_decay * m[j, :, :, :, :, cols].reshape(256, TILE) + grad) * use
            new_momentum[j, :, cols] = moved
            new_weights[j, :, cols] = (
                w[j, :, :, :, :, cols].reshape(256, TILE)
                - outer_rate * (grad + momentum_decay * moved)
            ) * use
            return carry

        lax.fori_loop(0, D // TILE, owner_body, 0)
        if j == 0:
            for i in range(7, 15):
                side_step(i)

    for i in range(FIRST, 15):
        swap_step(i)
    own_copy.wait()
    for i in range(32):
        send(r.at[0, 0], r.at[other, 0], swap_send, swap_recv.at[i], partner).wait_recv()

    flat = r.at[0]
    send(flat.at[pl.ds(0, 15)], flat.at[pl.ds(0, 15)], far_send, far_recv.at[0], up).wait_send()
    send(relay.at[pl.ds(0, 15)], relay.at[pl.ds(0, 15)], relay_send, far_recv.at[0], up).wait_send()
    send(flat.at[pl.ds(0, 16)], flat.at[pl.ds(0, 16)], side_send, far_recv.at[0], up).wait_send()
    send(flat, flat, swap_send, far_recv.at[0], up).wait_send()
    tiles.wait_send()
    for copy in part_copies:
        copy.wait_send()


def finish(new_weights_v, new_momentum_v, r, og, slots_v, new_weights, new_momentum, replica,
           rows, slots, sem, slot_sem):
    slot_copy = pltpu.make_async_copy(slots_v, slots, slot_sem)
    slot_copy.start()
    pairs = []
    for a, b in ((new_weights_v, new_weights), (new_momentum_v, new_momentum)):
        pairs += [
            (a.at[s, pl.ds(h * 128, 128)], b.at[s, pl.ds(h * 128, 128)])
            for s in range(2) for h in range(2)
        ]
    pairs += [(rows.at[pl.ds(g * 8, 8)], replica.at[pl.ds(g * 8, 8)]) for g in range(4)]
    copies = [pltpu.make_async_copy(a, b, sem.at[i]) for i, (a, b) in enumerate(pairs)]
    for copy in copies[:8]:
        copy.start()
    slot_copy.wait()

    def out_body(b, carry):
        slot = slots[0, b]
        for half in range(2):
            cols = slice(half * HALF, (half + 1) * HALF)
            rows[b, :, cols] = r[half, slot // 2, slot % 2] - (
                outer_rate * (1.0 + momentum_decay)
            ) * og[pl.ds(pl.multiple_of(b * 8, 8), 8), cols]
        return carry

    for g in range(4):
        lax.fori_loop(g * 8, g * 8 + 8, out_body, 0)
        if g > 0:
            copies[8 + g - 1].start()
    copies[11].start()
    for copy in copies:
        copy.wait()


def local(replica_delta, layer_basis, layer_of, owner_of, weights_owned, momentum_owned):
    vmem = pl.BlockSpec(memory_space=pltpu.VMEM)
    hbm = pl.BlockSpec(memory_space=pltpu.HBM)
    dma = pltpu.SemaphoreType.DMA
    basis = jnp.swapaxes(layer_basis, 1, 2).reshape(4 * RANK, D)
    delta = replica_delta.reshape(256, D)
    weights = weights_owned.reshape(2, 2, 4, 4, 8, D)
    momentum = momentum_owned.reshape(2, 2, 4, 4, 8, D)
    between = pl.pallas_call(
        exchange,
        out_shape=(
            pltpu.VMEM((2, 256, D), F32),
            pltpu.VMEM((2, 256, D), F32),
            pltpu.VMEM((2, OWN, 2, 8, HALF), F32),
            pltpu.VMEM((256, D), F32),
            pltpu.VMEM((1, 128), jnp.int32),
        ),
        in_specs=[hbm] * 6,
        out_specs=(vmem,) * 5,
        scratch_shapes=[
            pltpu.VMEM((1, BLOCKS), jnp.int32),
            pltpu.VMEM((1, BLOCKS), jnp.int32),
            pltpu.VMEM((2, 2, 4, 4, 8, D), F32),
            pltpu.VMEM((2, 2, 4, 4, 8, D), F32),
            pltpu.VMEM((256, D), F32),
            pltpu.VMEM((256, D), F32),
            pltpu.VMEM((256, D), BF16),
            pltpu.VMEM((256, D), BF16),
            pltpu.VMEM((2, 4, 4, 2, 8, HALF), F32),
            pltpu.VMEM((16, 8, HALF), F32),
            pltpu.VMEM((4, 128, 128), F32),
            pltpu.VMEM((OWN, 8, 128), F32),
            pltpu.VMEM((OWN, 8, 128), F32),
            dma((12,)),
            dma, dma((15,)),
            dma, dma((15,)),
            dma, dma((2, 16)),
            dma, dma((32,)),
            dma((3,)), dma((3,)),
            dma, dma,
            dma((2,)),
            dma((2,)),
        ],
        compiler_params=pltpu.CompilerParams(
            collective_id=0, has_side_effects=True, vmem_limit_bytes=40 << 20
        ),
        name="outer_step",
    )(owner_of.reshape(1, BLOCKS), layer_of.reshape(1, BLOCKS), delta, basis, weights, momentum)
    shapes = ((2, 256, D), (2, 256, D), (BLOCKS, 8, D))
    return pl.pallas_call(
        finish,
        out_shape=tuple(jax.ShapeDtypeStruct(shape, F32) for shape in shapes),
        in_specs=[vmem] * 5,
        out_specs=(hbm,) * 3,
        scratch_shapes=[
            pltpu.VMEM((BLOCKS, 8, D), F32), pltpu.SMEM((1, 128), jnp.int32), dma((12,)), dma,
        ],
        compiler_params=pltpu.CompilerParams(vmem_limit_bytes=24 << 20),
        name="finish",
    )(*between)


def solution(mesh):
    placed = (
        P("rep", None, "own", None),
        P(),
        P(),
        P(),
        P("own", None, None),
        P("own", None, None),
    )
    return jax.shard_map(
        local,
        mesh=mesh,
        in_specs=placed,
        out_specs=(P("own", None, None), P("own", None, None), P(None, "own", None)),
        check_vma=False,
    )
```

time: 284 us -> 39.4 us (0.14)
  waiting for transfers between devices: 149 us -> 0 us
  local copies, waits for them, and re-layouts: 53.6 us -> 1.3 us
  Pallas kernels: 0 us -> 37.3 us
  matrix products: 33 us -> 0 us
  starting transfers between devices: 32.2 us -> 0 us
  between operations: 14.2 us -> 0.65 us
    all_to_all x4 -> x0, waiting for transfers between devices: 142 us -> none  [the longest x1 42 us: local(): lax.all_to_all(placed_weights, 'own', split_axis=0, concat_axis=1, tiled=...]
    pallas_call x0 -> x2, Pallas kernels: none -> 37.3 us  [the longest x1 33.6 us: local(): pl.pallas_call(exchange, out_shape=(pltpu.VMEM((2, 256, D), F32), pltpu.V...]
    dot_general x4 -> x0, matrix products: 33 us -> none  [the longest x1 17 us: local(): jnp.einsum('bnd,bdk->bnk', replica_delta[0], chosen, precision=highest)]
    all_to_all x4 -> x0, starting transfers between devices: 32 us -> none  [the longest x1 9.93 us: local(): lax.all_to_all(weights_owned, 'own', split_axis=1, concat_axis=0, tiled=T...]
    all_to_all x6 -> x0, local copies, waits for them, and re-layouts: 17.5 us -> none  [the longest x2 4.56 us: local(): lax.all_to_all(weights_owned, 'own', split_axis=1, concat_axis=0, tiled=T...]
    gather x3 -> x0, local copies, waits for them, and re-layouts: 14.6 us -> none  [the longest x1 6.68 us: local(): chosen = jnp.take(layer_basis, layer_of, axis=0)]
    unnamed x12 -> x4, local copies, waits for them, and re-layouts: 13.6 us -> 1.3 us
    dot_general x2 -> x0, local copies, waits for them, and re-layouts: 7.93 us -> none  [the longest x1 3.96 us: local(): jnp.einsum('sb,bnd->snd', holding, momentum_next, precision=highest)]
  transfers between devices with their start and end apart: 5 -> 0, of which waited for: 5 -> 0; matrix products, arithmetic and copies ran while one was open for 21% -> 0% of each run, Pallas kernels for 0% -> 0%
where the time goes in v2:
time: 39.4 us; the launch traced here: 39.2 us
  Pallas kernels  37.3 us (95%)
  local copies, waits for them, and re-layouts  1.3 us (3%)
  between operations  0.65 us (2%)
    pallas_call x1, Pallas kernels, local(): pl.pallas_call(exchange, out_shape=(pltpu.VMEM((2, 256, D), F32), pltpu.V...  33.6 us
    pallas_call x1, Pallas kernels, local(): pl.pallas_call(finish, out_shape=tuple((jax.ShapeDtypeStruct(shape, F32)...  3.64 us
    unnamed x4, local copies, waits for them, and re-layouts  1.3 us

profile of v2, /device:TPU:1, one launch (start us, length us, event | category | flops | bytes accessed | tf_op | source)
XLA Modules:
  0.0 39.2 jit_solution(4351330528337493658)
XLA Ops:
  0.6 0.0 copy-start
  0.6 0.6 %copy-done = s32[32]{0:T(128)S(1)} copy-done((s32[32]{0:T(128)S(1)}, s32[32]{0:T(128)}, u32[]{:S(2)}) %copy-start) | copy-done | bytes 152
  1.3 0.0 copy-start.1
  1.3 0.7 %copy-done.1 = s32[32]{0:T(128)S(1)} copy-done((s32[32]{0:T(128)S(1)}, s32[32]{0:T(128)}, u32[]{:S(2)}) %copy-start.1) | copy-done | bytes 152
  1.9 33.6 %outer_step.1 = (f32[2,256,1792]{2,1,0:T(8,128)S(1)}, f32[2,256,1792]{2,1,0:T(8,128)S(1)}, f32[2,32,2,8,896]{4,3,2,1,0:T(8,128)S(1)}, f32[256,1792]{1,0:T(8,128)S(1)}, s32[1,128]{1,0:T(1,128)S(1)}) custom-call(s32[1,32]{1,0:T(1,128)S(1)} %bitcast.8, s32[1,32]{1,0:T(1,128)S(1)} %bitcast.9, f32[256,1792]{1,0:T(8,128)} %bitcast.12, f32[256,1792]{1,0:T(8,128)} %bitcast.13, ...), custom_call_target="tpu_custom_call" | custom-call | tf_op jit(solution)/shard_map/outer_step/pallas_call | solution.py:378
  35.6 3.6 %finish.1 = (f32[2,256,1792]{2,1,0:T(8,128)}, f32[2,256,1792]{2,1,0:T(8,128)}, f32[32,8,1792]{2,1,0:T(8,128)}) custom-call(f32[2,256,1792]{2,1,0:T(8,128)S(1)} %get-tuple-element.8.new_weights_v, f32[2,256,1792]{2,1,0:T(8,128)S(1)} %get-tuple-element.9.new_momentum_v, f32[2,32,2,8,896]{4,3,2,1,0:T(8,128)S(1)} %get-tuple-element.10.r, ...), custom_call_target="tpu_custom_call" | custom-call | tf_op jit(solution)/shard_map/finish/pallas_call | solution.py:419
Async XLA Ops:
  0.6 0.7 %copy-start = (s32[32]{0:T(128)S(1)}, s32[32]{0:T(128)}, u32[]{:S(2)}) copy-start(s32[32]{0:T(128)} %param.9) | copy-start | bytes 388
  1.3 0.7 %copy-start.1 = (s32[32]{0:T(128)S(1)}, s32[32]{0:T(128)}, u32[]{:S(2)}) copy-start(s32[32]{0:T(128)} %param.8) | copy-start | bytes 388

commit v3 on v2

--- a/solution.py
+++ b/solution.py
@@ -23,7 +23,10 @@
 NEAR = [(1, 0), (3, 0), (2, 0)] + [(dy, dz) for dz in DZ[1:] for dy in (0, 1, 3, 2)]
 FAR = [(1, 2), (3, 2), (2, 1), (2, 3), (1, 1), (3, 3), (1, 3), (3, 1), (2, 2),
        (2, 0), (0, 2), (1, 0), (0, 1), (3, 0), (0, 3)]
-FIRST = 6
+FIRST = 10
+PASSES = [("side", 15)] + [("side", i) for i in range(5)] + [("swap", i) for i in range(5)]
+PASSES += [("side", i) for i in range(5, 10)] + [("swap", i) for i in range(5, 10)]
+PASSES += [("side", i) for i in range(10, 15)] + [("swap", i) for i in range(10, 15)]
 
 
 def place():
@@ -55,8 +58,8 @@
 
 def exchange(
     owner_hbm, layer_hbm, delta_hbm, basis_hbm, weights_hbm, momentum_hbm,
-    new_weights, new_momentum, r, og, slots,
-    owner_v, layer_v, w, m, d, bt, bt_high, bt_low, q, relay, parts, packed, placed,
+    w, m, r, og, placed, terms, table,
+    owner_v, layer_v, d, bt, q, relay, parts, packed,
     load_sem, far_send, far_recv, relay_send, relay_recv, side_send, side_recv,
     swap_send, swap_recv, part_send, part_recv, packed_send, packed_recv, own_sem,
     table_sem,
@@ -120,7 +123,13 @@
     slot_col = owner_col * 2 + jnp.sum(
         jnp.where(same & (lane32 < blk_col), 1, 0), axis=1, keepdims=True
     )
-    slots[...] = jnp.sum(jnp.where(blk_col == lane128, slot_col, 0), axis=0, keepdims=True)
+    layer_blk = jnp.sum(jnp.where(blk_col == lane32, layer_row, 0), axis=1, keepdims=True)
+    entry = jnp.where(blk_col == lane128, slot_col, 0)
+    for j in range(2):
+        hit = slot_col == me * 2 + j
+        entry = entry + jnp.where(hit & (lane128 == 32 + j), layer_blk, 0)
+        entry = entry + jnp.where(hit & (lane128 == 34 + j), 1, 0)
+    table[...] = jnp.sum(entry, axis=0, keepdims=True)
 
     def q_rows(k):
         tz = (z + DZ[k]) % 4
@@ -176,7 +185,13 @@
     copies[8].wait()
     for t in range(D // TILE):
         cols = slice(t * TILE, (t + 1) * TILE)
-        bt_high[:, cols], bt_low[:, cols] = split(bt[:, cols])
+        high, low_part = split(bt[:, :, cols])
+        for k, term in enumerate((high, low_part, high, low_part)):
+            terms[:, k * RANK:(k + 1) * RANK, cols] = term
+
+    def basis_terms(cols):
+        return [terms[:, k * RANK:(k + 1) * RANK, cols].reshape(256, TILE) for k in range(2)]
+
     for copy in onward[11:] + direct[:FIRST]:
         copy.start()
     copies[9].wait()
@@ -185,26 +200,20 @@
         cols = slice(t * TILE, (t + 1) * TILE)
         high, low_part = split(d[:, cols])
         along = ((1,), (1,))
+        bt_high, bt_low = basis_terms(cols)
         every = every + (
-            dot(high, bt_high[:, cols], along)
-            + (dot(high, bt_low[:, cols], along) + dot(low_part, bt_high[:, cols], along))
+            dot(high, bt_high, along) + (dot(high, bt_low, along) + dot(low_part, bt_high, along))
         )
     every = jnp.where(in_layer, every, 0.0)
     both = every[:, :128] + every[:, 128:]
     both = both + pltpu.roll(both, RANK, 1)
     parts[rep] = jnp.where(low, both[:128], both[128:])
 
-    layer_blk = jnp.sum(jnp.where(blk_col == lane32, layer_row, 0), axis=1, keepdims=True)
     slot_lane = jnp.sum(jnp.where(lane256 // 8 == blk_col, slot_col, 0), axis=0, keepdims=True)
     same_row = (row % 8) == (lane256 % 8)
     pick = [
         jnp.where(((row // 8) * 2 + j == slot_lane) & same_row, 1.0, 0.0) for j in range(2)
     ]
-    used, layers = [], []
-    for j in range(2):
-        hit = slot_col == me * 2 + j
-        used.append(jnp.sum(jnp.where(hit, 1.0, 0.0), axis=0, keepdims=True))
-        layers.append(jnp.sum(jnp.where(hit, layer_blk, 0), axis=0, keepdims=True))
 
     part_copies = [
         send(parts.at[rep], parts.at[rep], part_send.at[k], part_recv.at[k], to)
@@ -277,48 +286,18 @@
 
     def og_body(t, carry):
         cols = pl.ds(pl.multiple_of(t * TILE, TILE), TILE)
-        high = bt_high[:, cols]
-        og[:, cols] = dot(og_high, high) + (dot(og_high, bt_low[:, cols]) + dot(og_low, high))
+        bt_high, bt_low = basis_terms(cols)
+        og[:, cols] = dot(og_high, bt_high) + (dot(og_high, bt_low) + dot(og_low, bt_high))
         return carry
 
     lax.fori_loop(0, D // TILE, og_body, 0)
-    for i in (15, *range(7)):
-        side_step(i)
-    for i in range(FIRST):
-        swap_step(i)
-
+    for kind, i in PASSES:
+        (side_step if kind == "side" else swap_step)(i)
     own_packed.wait()
     tiles = send(packed.at[pl.ds(0, 31)], placed.at[pl.ds(0, 31)], packed_send, packed_recv, up)
     tiles.wait_recv()
     copies[10].wait()
     copies[11].wait()
-    got = placed[...].reshape(256, 128)
-    got_turned = pltpu.roll(got, RANK, 1)
-    for j in range(2):
-        pairs = jnp.where(low, got, got_turned) if j == 0 else jnp.where(low, got_turned, got)
-        in_slot = jnp.broadcast_to((lane256 // RANK) == layers[j], (256, 256))
-        slot_high, slot_low = split(spread(pairs, in_slot))
-        use = used[j]
-
-        def owner_body(t, carry, j=j, slot_high=slot_high, slot_low=slot_low, use=use):
-            cols = pl.ds(pl.multiple_of(t * TILE, TILE), TILE)
-            high = bt_high[:, cols]
-            grad = dot(slot_high, high) + (dot(slot_high, bt_low[:, cols]) + dot(slot_low, high))
-            moved = (momentum_decay * m[j, :, :, :, :, cols].reshape(256, TILE) + grad) * use
-            new_momentum[j, :, cols] = moved
-            new_weights[j, :, cols] = (
-                w[j, :, :, :, :, cols].reshape(256, TILE)
-                - outer_rate * (grad + momentum_decay * moved)
-            ) * use
-            return carry
-
-        lax.fori_loop(0, D // TILE, owner_body, 0)
-        if j == 0:
-            for i in range(7, 15):
-                side_step(i)
-
-    for i in range(FIRST, 15):
-        swap_step(i)
     own_copy.wait()
     for i in range(32):
         send(r.at[0, 0], r.at[other, 0], swap_send, swap_recv.at[i], partner).wait_recv()
@@ -333,24 +312,49 @@
         copy.wait_send()
 
 
-def finish(new_weights_v, new_momentum_v, r, og, slots_v, new_weights, new_momentum, replica,
-           rows, slots, sem, slot_sem):
-    slot_copy = pltpu.make_async_copy(slots_v, slots, slot_sem)
-    slot_copy.start()
-    pairs = []
-    for a, b in ((new_weights_v, new_weights), (new_momentum_v, new_momentum)):
-        pairs += [
-            (a.at[s, pl.ds(h * 128, 128)], b.at[s, pl.ds(h * 128, 128)])
-            for s in range(2) for h in range(2)
-        ]
-    pairs += [(rows.at[pl.ds(g * 8, 8)], replica.at[pl.ds(g * 8, 8)]) for g in range(4)]
-    copies = [pltpu.make_async_copy(a, b, sem.at[i]) for i, (a, b) in enumerate(pairs)]
-    for copy in copies[:8]:
-        copy.start()
-    slot_copy.wait()
+def finish(
+    w, m, r, og, placed, terms, table_v, new_weights, new_momentum, replica,
+    moved_w, moved_m, rows, table, sem, row_sem, table_sem,
+):
+    table_copy = pltpu.make_async_copy(table_v, table, table_sem)
+    table_copy.start()
+    got = placed[...].reshape(256, 128)
+    got_turned = pltpu.roll(got, RANK, 1)
+    low = lax.broadcasted_iota(jnp.int32, (1, 128), 1) < RANK
+    sides = []
+    for j in range(2):
+        pairs = jnp.where(low, got, got_turned) if j == 0 else jnp.where(low, got_turned, got)
+        sides.append(jnp.concatenate(split(pairs), axis=1))
+    table_copy.wait()
+
+    copies = []
+
+    def issue(k):
+        for copy in copies[2 * k:2 * k + 2]:
+            copy.start()
+
+    for j in range(2):
+        layer = table[0, 32 + j]
+        use = table[0, 34 + j].astype(F32)
+        for t in range(D // TILE):
+            cols = slice(t * TILE, (t + 1) * TILE)
+            k = j * (D // TILE) + t
+            grad = dot(sides[j], terms[layer, :, cols])
+            moved = (momentum_decay * m[j, :, :, :, :, cols].reshape(256, TILE) + grad) * use
+            moved_m[j, :, cols] = moved
+            moved_w[j, :, cols] = (
+                w[j, :, :, :, :, cols].reshape(256, TILE)
+                - outer_rate * (grad + momentum_decay * moved)
+            ) * use
+            copies.append(pltpu.make_async_copy(
+                moved_m.at[j, :, cols], new_momentum.at[j, :, cols], sem.at[0, k]))
+            copies.append(pltpu.make_async_copy(
+                moved_w.at[j, :, cols], new_weights.at[j, :, cols], sem.at[1, k]))
+            if k > 0:
+                issue(k - 1)
 
     def out_body(b, carry):
-        slot = slots[0, b]
+        slot = table[0, b]
         for half in range(2):
             cols = slice(half * HALF, (half + 1) * HALF)
             rows[b, :, cols] = r[half, slot // 2, slot % 2] - (
@@ -358,12 +362,18 @@
             ) * og[pl.ds(pl.multiple_of(b * 8, 8), 8), cols]
         return carry
 
+    row_copies = [
+        pltpu.make_async_copy(rows.at[pl.ds(g * 8, 8)], replica.at[pl.ds(g * 8, 8)], row_sem.at[g])
+        for g in range(4)
+    ]
     for g in range(4):
         lax.fori_loop(g * 8, g * 8 + 8, out_body, 0)
-        if g > 0:
-            copies[8 + g - 1].start()
-    copies[11].start()
-    for copy in copies:
+        if g == 0:
+            issue(2 * (D // TILE) - 1)
+        else:
+            row_copies[g - 1].start()
+    row_copies[3].start()
+    for copy in copies + row_copies:
         copy.wait()
 
 
@@ -371,34 +381,31 @@
     vmem = pl.BlockSpec(memory_space=pltpu.VMEM)
     hbm = pl.BlockSpec(memory_space=pltpu.HBM)
     dma = pltpu.SemaphoreType.DMA
-    basis = jnp.swapaxes(layer_basis, 1, 2).reshape(4 * RANK, D)
+    basis = jnp.swapaxes(layer_basis, 1, 2)
     delta = replica_delta.reshape(256, D)
     weights = weights_owned.reshape(2, 2, 4, 4, 8, D)
     momentum = momentum_owned.reshape(2, 2, 4, 4, 8, D)
     between = pl.pallas_call(
         exchange,
         out_shape=(
-            pltpu.VMEM((2, 256, D), F32),
-            pltpu.VMEM((2, 256, D), F32),
+            pltpu.VMEM((2, 2, 4, 4, 8, D), F32),
+            pltpu.VMEM((2, 2, 4, 4, 8, D), F32),
             pltpu.VMEM((2, OWN, 2, 8, HALF), F32),
             pltpu.VMEM((256, D), F32),
+            pltpu.VMEM((OWN, 8, 128), F32),
+            pltpu.VMEM((4, 4 * RANK, D), BF16),
             pltpu.VMEM((1, 128), jnp.int32),
         ),
         in_specs=[hbm] * 6,
-        out_specs=(vmem,) * 5,
+        out_specs=(vmem,) * 7,
         scratch_shapes=[
             pltpu.VMEM((1, BLOCKS), jnp.int32),
             pltpu.VMEM((1, BLOCKS), jnp.int32),
-            pltpu.VMEM((2, 2, 4, 4, 8, D), F32),
-            pltpu.VMEM((2, 2, 4, 4, 8, D), F32),
             pltpu.VMEM((256, D), F32),
-            pltpu.VMEM((256, D), F32),
-            pltpu.VMEM((256, D), BF16),
-            pltpu.VMEM((256, D), BF16),
+            pltpu.VMEM((4, RANK, D), F32),
             pltpu.VMEM((2, 4, 4, 2, 8, HALF), F32),
             pltpu.VMEM((16, 8, HALF), F32),
             pltpu.VMEM((4, 128, 128), F32),
-            pltpu.VMEM((OWN, 8, 128), F32),
             pltpu.VMEM((OWN, 8, 128), F32),
             dma((12,)),
             dma, dma((15,)),
@@ -411,7 +418,7 @@
             dma((2,)),
         ],
         compiler_params=pltpu.CompilerParams(
-            collective_id=0, has_side_effects=True, vmem_limit_bytes=40 << 20
+            collective_id=0, has_side_effects=True, vmem_limit_bytes=45 << 20
         ),
         name="outer_step",
     )(owner_of.reshape(1, BLOCKS), layer_of.reshape(1, BLOCKS), delta, basis, weights, momentum)
@@ -419,12 +426,14 @@
     return pl.pallas_call(
         finish,
         out_shape=tuple(jax.ShapeDtypeStruct(shape, F32) for shape in shapes),
-        in_specs=[vmem] * 5,
+        in_specs=[vmem] * 7,
         out_specs=(hbm,) * 3,
         scratch_shapes=[
-            pltpu.VMEM((BLOCKS, 8, D), F32), pltpu.SMEM((1, 128), jnp.int32), dma((12,)), dma,
+            pltpu.VMEM((2, 256, D), F32), pltpu.VMEM((2, 256, D), F32),
+            pltpu.VMEM((BLOCKS, 8, D), F32), pltpu.SMEM((1, 128), jnp.int32),
+            dma((2, 14)), dma((4,)), dma,
         ],
-        compiler_params=pltpu.CompilerParams(vmem_limit_bytes=24 << 20),
+        compiler_params=pltpu.CompilerParams(vmem_limit_bytes=16 << 20),
         name="finish",
     )(*between)
 

time: 39.4 us -> 35.5 us (0.901)
  Pallas kernels: 37.3 us -> 34.8 us
  local copies, waits for them, and re-layouts: 1.3 us -> 0 us
    pallas_call x1, Pallas kernels: 33.6 us -> 30.1 us  [local(): pl.pallas_call(exchange, out_shape=(pltpu.VMEM((2, 2, 4, 4, 8, D), F32),...]
    unnamed x4 -> x0, local copies, waits for them, and re-layouts: 1.3 us -> none
    pallas_call x1, Pallas kernels: 3.64 us -> 4.66 us  [local(): pl.pallas_call(finish, out_shape=tuple((jax.ShapeDtypeStruct(shape, F32)...]
where the time goes in v3:
time: 35.5 us; the launch traced here: 35.4 us
  Pallas kernels  34.8 us (98%)
  between operations  0.64 us (2%)
    pallas_call x1, Pallas kernels, local(): pl.pallas_call(exchange, out_shape=(pltpu.VMEM((2, 2, 4, 4, 8, D), F32),...  30.1 us
    pallas_call x1, Pallas kernels, local(): pl.pallas_call(finish, out_shape=tuple((jax.ShapeDtypeStruct(shape, F32)...  4.66 us

profile of v3, /device:TPU:1, one launch (start us, length us, event | category | flops | bytes accessed | tf_op | source)
XLA Modules:
  0.0 35.4 jit_solution(5004618823320522821)
XLA Ops:
  0.6 30.1 %outer_step.1 = (f32[2,2,4,4,8,1792]{5,4,3,2,1,0:T(8,128)S(1)}, f32[2,2,4,4,8,1792]{5,4,3,2,1,0:T(8,128)S(1)}, f32[2,32,2,8,896]{4,3,2,1,0:T(8,128)S(1)}, f32[25...) custom-call(s32[1,32]{1,0:T(1,128)} %bitcast.10, ...), custom_call_target="tpu_custom_call" | custom-call | tf_op jit(solution)/shard_map/outer_step/pallas_call | solution.py:388
  30.8 4.7 %finish.1 = (f32[2,256,1792]{2,1,0:T(8,128)}, f32[2,256,1792]{2,1,0:T(8,128)}, f32[32,8,1792]{2,1,0:T(8,128)}) custom-call(f32[2,2,4,4,8,1792]{5,4,3,2,1,0:T(8,128)S(1)} %get-tuple-element.10.w, f32[2,2,4,4,8,1792]{5,4,3,2,1,0:T(8,128)S(1)} %get-tuple-element.11.m, f32[2,32,2,8,896]{4,3,2,1,0:T(8,128)S(1)} %get-tuple-element.12.r, ...), custom_call_target="tpu_custom_call" | custom-call | tf_op jit(solution)/shard_map/finish/pallas_call | solution.py:426

commit v4 on v3

--- a/solution.py
+++ b/solution.py
@@ -20,13 +20,18 @@
 F32 = jnp.float32
 
 DZ = [0, 1, 3, 2]
-NEAR = [(1, 0), (3, 0), (2, 0)] + [(dy, dz) for dz in DZ[1:] for dy in (0, 1, 3, 2)]
-FAR = [(1, 2), (3, 2), (2, 1), (2, 3), (1, 1), (3, 3), (1, 3), (3, 1), (2, 2),
-       (2, 0), (0, 2), (1, 0), (0, 1), (3, 0), (0, 3)]
-FIRST = 10
-PASSES = [("side", 15)] + [("side", i) for i in range(5)] + [("swap", i) for i in range(5)]
-PASSES += [("side", i) for i in range(5, 10)] + [("swap", i) for i in range(5, 10)]
-PASSES += [("side", i) for i in range(10, 15)] + [("swap", i) for i in range(10, 15)]
+NEAR = [(1, 0), (3, 0), (0, 1), (0, 3),
+        (2, 0), (1, 1), (3, 3), (3, 1), (1, 3), (0, 2),
+        (1, 2), (3, 2), (2, 1), (2, 3), (2, 2)]
+FAR = [(1, 0), (3, 0), (0, 1), (0, 3),
+       (2, 2), (1, 2), (3, 2), (2, 1), (2, 3),
+       (1, 1), (3, 3), (3, 1), (1, 3), (2, 0), (0, 2)]
+FIRST = 9
+PASSES = [("swap", i) for i in range(4)] + [("side", 15)] + [("side", i) for i in range(4)]
+PASSES += [("side", i) for i in range(4, 8)]
+PASSES += [("swap", i) for i in range(4, 9)] + [("side", i) for i in range(8, 12)]
+PASSES += [("swap", i) for i in range(9, 12)]
+PASSES += [("side", i) for i in range(12, 15)] + [("swap", i) for i in range(12, 15)]
 
 
 def place():
@@ -74,6 +79,15 @@
     partner = device(x, y, z, other)
     peers = [partner, device(x_far, y, z, core), device(x_far, y, z, other)]
 
+    barrier = pltpu.get_barrier_semaphore()
+    targets = []
+    for dy, dz in reversed(NEAR):
+        for tx in (hi * 2 + 1 - lo, x):
+            targets.append(device(tx, (y + dy) % 4, (z + dz) % 4, core))
+    targets += peers + [up, down]
+    for to in targets:
+        pl.semaphore_signal(barrier, inc=1, device_id=to, device_id_type=MESH)
+
     tables = [
         pltpu.make_async_copy(a, b, table_sem.at[i])
         for i, (a, b) in enumerate(((owner_hbm, owner_v), (layer_hbm, layer_v)))
@@ -98,13 +112,85 @@
     for copy in copies:
         copy.start()
 
-    barrier = pltpu.get_barrier_semaphore()
-    targets = [up, down] + peers
-    for dy, dz in FAR:
-        for tx in (x, hi * 2 + 1 - lo):
-            targets.append(device(tx, (y + dy) % 4, (z + dz) % 4, core))
-    for to in targets:
-        pl.semaphore_signal(barrier, inc=1, device_id=to, device_id_type=MESH)
+    def q_rows(k):
+        tz = (z + DZ[k]) % 4
+        copies[2 * k].wait()
+        copies[2 * k + 1].wait()
+        for half in range(2):
+            @pl.when(core == half)
+            def _():
+                cols = slice(half * HALF, (half + 1) * HALF)
+                for s in range(2):
+                    q[:, tz, :, s] = w[s, :, tz, :, :, cols] - (
+                        outer_rate * momentum_decay * momentum_decay
+                    ) * m[s, :, tz, :, :, cols]
+
+    def direct_copy(i):
+        dy, dz = FAR[i]
+        ty, tz = (y + dy) % 4, (z + dz) % 4
+        return send(
+            q.at[lo, tz, ty], r.at[core, me], far_send, far_recv.at[i], device(x, ty, tz, core)
+        )
+
+    def onward_copy(i):
+        dy, dz = NEAR[i]
+        ty, tz = (y + dy) % 4, (z + dz) % 4
+        return send(
+            q.at[1 - lo, tz, ty, hi], relay.at[z * 4 + y], relay_send, relay_recv.at[i],
+            device(x, ty, tz, core),
+        )
+
+    onward = [onward_copy(i) for i in range(15)]
+    direct = [direct_copy(i) for i in range(15)]
+    own_copy = pltpu.make_async_copy(q.at[lo, z, y], r.at[core, me], own_sem.at[0])
+    own_swap = send(q.at[lo, z, y], r.at[core, me], swap_send, swap_recv.at[15], partner)
+    side = [
+        send(q.at[1 - lo, z, y, hi], r.at[core, me, hi], side_send, side_recv.at[k, 15], to)
+        for k, to in enumerate((up, down))
+    ]
+
+    q_rows(0)
+    q_rows(1)
+    pl.semaphore_wait(barrier, len(targets))
+    for copy in side + onward[:2] + direct[:2]:
+        copy.start()
+    q_rows(2)
+    for copy in (onward[2], direct[2]):
+        copy.start()
+    q_rows(3)
+    for copy in (onward[3], direct[3]):
+        copy.start()
+    for copy in onward[4:10]:
+        copy.start()
+    for copy in onward[10:14]:
+        copy.start()
+    own_copy.start()
+    own_swap.start()
+
+    def source(dy, dz):
+        return (y + 4 - dy) % 4, (z + 4 - dz) % 4
+
+    def onward_step(i):
+        fy, fz = source(*NEAR[i])
+        src = lo * 16 + fz * 4 + fy
+        onward[i].wait_recv()
+        for k, to in enumerate((up, down)):
+            send(relay.at[fz * 4 + fy], r.at[core, src, hi], side_send, side_recv.at[k, i], to).start()
+
+    def swap_step(i):
+        fy, fz = source(*FAR[i])
+        src = lo * 16 + fz * 4 + fy
+        direct[i].wait_recv()
+        send(r.at[core, src], r.at[core, src], swap_send, swap_recv.at[i], partner).start()
+
+    def side_step(i):
+        fy, fz = source(*(NEAR[i] if i < 15 else (0, 0)))
+        src = (1 - lo) * 16 + fz * 4 + fy
+        for k, from_x in enumerate((x_down, x_up)):
+            send(
+                relay.at[0], r.at[core, src, from_x // 2], side_send, side_recv.at[k, i], up
+            ).wait_recv()
+        send(r.at[core, src], r.at[core, src], swap_send, swap_recv.at[16 + i], partner).start()
 
     row = lax.broadcasted_iota(jnp.int32, (256, 1), 0)
     lane256 = lax.broadcasted_iota(jnp.int32, (1, 256), 1)
@@ -131,57 +217,6 @@
         entry = entry + jnp.where(hit & (lane128 == 34 + j), 1, 0)
     table[...] = jnp.sum(entry, axis=0, keepdims=True)
 
-    def q_rows(k):
-        tz = (z + DZ[k]) % 4
-        copies[2 * k].wait()
-        copies[2 * k + 1].wait()
-        for half in range(2):
-            @pl.when(core == half)
-            def _():
-                cols = slice(half * HALF, (half + 1) * HALF)
-                for s in range(2):
-                    q[:, tz, :, s] = w[s, :, tz, :, :, cols] - (
-                        outer_rate * momentum_decay * momentum_decay
-                    ) * m[s, :, tz, :, :, cols]
-
-    def direct_copy(i):
-        dy, dz = FAR[i]
-        ty, tz = (y + dy) % 4, (z + dz) % 4
-        return send(
-            q.at[lo, tz, ty], r.at[core, me], far_send, far_recv.at[i], device(x, ty, tz, core)
-        )
-
-    def onward_copy(i):
-        dy, dz = NEAR[i]
-        ty, tz = (y + dy) % 4, (z + dz) % 4
-        return send(
-            q.at[1 - lo, tz, ty, hi], relay.at[z * 4 + y], relay_send, relay_recv.at[i],
-            device(x, ty, tz, core),
-        )
-
-    onward = [onward_copy(i) for i in range(15)]
-    direct = [direct_copy(i) for i in range(15)]
-    own_copy = pltpu.make_async_copy(q.at[lo, z, y], r.at[core, me], own_sem.at[0])
-    own_swap = send(q.at[lo, z, y], r.at[core, me], swap_send, swap_recv.at[15], partner)
-    side = [
-        send(q.at[1 - lo, z, y, hi], r.at[core, me, hi], side_send, side_recv.at[k, 15], to)
-        for k, to in enumerate((up, down))
-    ]
-
-    q_rows(0)
-    q_rows(1)
-    pl.semaphore_wait(barrier, len(targets))
-    for copy in side + onward[:3]:
-        copy.start()
-    q_rows(2)
-    for copy in onward[3:7]:
-        copy.start()
-    q_rows(3)
-    for copy in onward[7:11]:
-        copy.start()
-    own_copy.start()
-    own_swap.start()
-
     copies[8].wait()
     for t in range(D // TILE):
         cols = slice(t * TILE, (t + 1) * TILE)
@@ -192,7 +227,7 @@
     def basis_terms(cols):
         return [terms[:, k * RANK:(k + 1) * RANK, cols].reshape(256, TILE) for k in range(2)]
 
-    for copy in onward[11:] + direct[:FIRST]:
+    for copy in onward[14:] + direct[4:FIRST]:
         copy.start()
     copies[9].wait()
     every = jnp.zeros((256, 256), F32)
@@ -222,31 +257,6 @@
     for copy in part_copies[1:] + part_copies[:1]:
         copy.start()
 
-    def source(dy, dz):
-        return (y + 4 - dy) % 4, (z + 4 - dz) % 4
-
-    def onward_step(i):
-        fy, fz = source(*NEAR[i])
-        src = lo * 16 + fz * 4 + fy
-        onward[i].wait_recv()
-        for k, to in enumerate((up, down)):
-            send(relay.at[fz * 4 + fy], r.at[core, src, hi], side_send, side_recv.at[k, i], to).start()
-
-    def swap_step(i):
-        fy, fz = source(*FAR[i])
-        src = lo * 16 + fz * 4 + fy
-        direct[i].wait_recv()
-        send(r.at[core, src], r.at[core, src], swap_send, swap_recv.at[i], partner).start()
-
-    def side_step(i):
-        fy, fz = source(*(NEAR[i] if i < 15 else (0, 0)))
-        src = (1 - lo) * 16 + fz * 4 + fy
-        for k, from_x in enumerate((x_down, x_up)):
-            send(
-                relay.at[0], r.at[core, src, from_x // 2], side_send, side_recv.at[k, i], up
-            ).wait_recv()
-        send(r.at[core, src], r.at[core, src], swap_send, swap_recv.at[16 + i], partner).start()
-
     for i in range(9):
         onward_step(i)
     for copy in part_copies:
@@ -266,18 +276,31 @@
 
     og_high, og_low = split(spread(dup, in_layer))
 
+    takes = core == (lo + y + z + 1) % 2
+
+    def send_tiles(parity):
+        for dy, dz in NEAR[::-1] + [(0, 0)]:
+            for s in range(2):
+                if (dy + dz + s) % 2 != parity or (s == 0 and (dy, dz) == (0, 0)):
+                    continue
+                ty, tz = (y + dy) % 4, (z + dz) % 4
+                to_lo = lo if s == 0 else 1 - lo
+                send(
+                    packed.at[to_lo * 16 + tz * 4 + ty], placed.at[me], packed_send.at[0],
+                    packed_recv.at[0], device(hi * 2 + to_lo, ty, tz, core),
+                ).start()
+
     own_packed = pltpu.make_async_copy(packed.at[me], placed.at[me], own_sem.at[1])
-    own_packed.start()
-    for dy, dz in FAR + [(0, 0)]:
-        for s in range(2):
-            if s == 0 and (dy, dz) == (0, 0):
-                continue
-            ty, tz = (y + dy) % 4, (z + dz) % 4
-            to_lo = lo if s == 0 else 1 - lo
-            send(
-                packed.at[to_lo * 16 + tz * 4 + ty], placed.at[me], packed_send,
-                packed_recv, device(hi * 2 + to_lo, ty, tz, core),
-            ).start()
+
+    @pl.when(takes)
+    def _():
+        own_packed.start()
+        send_tiles(0)
+
+    @pl.when(jnp.logical_not(takes))
+    def _():
+        send_tiles(1)
+
     for copy in direct[FIRST:]:
         copy.start()
 
@@ -291,11 +314,29 @@
         return carry
 
     lax.fori_loop(0, D // TILE, og_body, 0)
-    for kind, i in PASSES:
-        (side_step if kind == "side" else swap_step)(i)
-    own_packed.wait()
-    tiles = send(packed.at[pl.ds(0, 31)], placed.at[pl.ds(0, 31)], packed_send, packed_recv, up)
-    tiles.wait_recv()
+    steps = {"side": side_step, "swap": swap_step}
+    hand_over = send(placed, placed, packed_send.at[1], packed_recv.at[1], partner)
+    tiles = [
+        send(packed.at[pl.ds(0, n)], placed.at[pl.ds(0, n)], packed_send.at[0], packed_recv.at[0], up)
+        for n in (15, 16, 31)
+    ]
+    late = 9
+    for kind, i in PASSES[:-late]:
+        steps[kind](i)
+
+    @pl.when(takes)
+    def _():
+        own_packed.wait()
+        tiles[2].wait_recv()
+        hand_over.start()
+
+    for kind, i in PASSES[-late:]:
+        steps[kind](i)
+
+    @pl.when(jnp.logical_not(takes))
+    def _():
+        hand_over.wait_recv()
+
     copies[10].wait()
     copies[11].wait()
     own_copy.wait()
@@ -307,9 +348,17 @@
     send(relay.at[pl.ds(0, 15)], relay.at[pl.ds(0, 15)], relay_send, far_recv.at[0], up).wait_send()
     send(flat.at[pl.ds(0, 16)], flat.at[pl.ds(0, 16)], side_send, far_recv.at[0], up).wait_send()
     send(flat, flat, swap_send, far_recv.at[0], up).wait_send()
-    tiles.wait_send()
     for copy in part_copies:
         copy.wait_send()
+
+    @pl.when(takes)
+    def _():
+        tiles[0].wait_send()
+        hand_over.wait_send()
+
+    @pl.when(jnp.logical_not(takes))
+    def _():
+        tiles[1].wait_send()
 
 
 def finish(
@@ -320,12 +369,12 @@
     table_copy.start()
     got = placed[...].reshape(256, 128)
     got_turned = pltpu.roll(got, RANK, 1)
-    low = lax.broadcasted_iota(jnp.int32, (1, 128), 1) < RANK
+    lane = lax.broadcasted_iota(jnp.int32, (1, 128), 1)
+    low = lane < RANK
     sides = []
     for j in range(2):
         pairs = jnp.where(low, got, got_turned) if j == 0 else jnp.where(low, got_turned, got)
         sides.append(jnp.concatenate(split(pairs), axis=1))
-    table_copy.wait()
 
     copies = []
 
@@ -334,8 +383,9 @@
             copy.start()
 
     for j in range(2):
-        layer = table[0, 32 + j]
-        use = table[0, 34 + j].astype(F32)
+        layer = jnp.sum(jnp.where(lane == 32 + j, table_v[...], 0))
+        use = jnp.where(lane == 34 + j, table_v[...], 0)
+        use = jnp.sum(use, axis=1, keepdims=True).astype(F32)
         for t in range(D // TILE):
             cols = slice(t * TILE, (t + 1) * TILE)
             k = j * (D // TILE) + t
@@ -366,6 +416,7 @@
         pltpu.make_async_copy(rows.at[pl.ds(g * 8, 8)], replica.at[pl.ds(g * 8, 8)], row_sem.at[g])
         for g in range(4)
     ]
+    table_copy.wait()
     for g in range(4):
         lax.fori_loop(g * 8, g * 8 + 8, out_body, 0)
         if g == 0:
@@ -413,7 +464,7 @@
             dma, dma((2, 16)),
             dma, dma((32,)),
             dma((3,)), dma((3,)),
-            dma, dma,
+            dma((2,)), dma((2,)),
             dma((2,)),
             dma((2,)),
         ],

time: 35.5 us -> 34.5 us (0.972)
  Pallas kernels: 34.8 us -> 33.8 us
    pallas_call x1, Pallas kernels: 30.1 us -> 29.5 us  [local(): pl.pallas_call(exchange, out_shape=(pltpu.VMEM((2, 2, 4, 4, 8, D), F32),...]
    pallas_call x1, Pallas kernels: 4.66 us -> 4.26 us  [local(): pl.pallas_call(finish, out_shape=tuple((jax.ShapeDtypeStruct(shape, F32)...]
where the time goes in v4:
time: 34.5 us; the launch traced here: 34.4 us
  Pallas kernels  33.8 us (98%)
  between operations  0.64 us (2%)
    pallas_call x1, Pallas kernels, local(): pl.pallas_call(exchange, out_shape=(pltpu.VMEM((2, 2, 4, 4, 8, D), F32),...  29.5 us
    pallas_call x1, Pallas kernels, local(): pl.pallas_call(finish, out_shape=tuple((jax.ShapeDtypeStruct(shape, F32)...  4.26 us

profile of v4, /device:TPU:1, one launch (start us, length us, event | category | flops | bytes accessed | tf_op | source)
XLA Modules:
  0.0 34.4 jit_solution(4021240408245082947)
XLA Ops:
  0.6 29.5 %outer_step.1 = (f32[2,2,4,4,8,1792]{5,4,3,2,1,0:T(8,128)S(1)}, f32[2,2,4,4,8,1792]{5,4,3,2,1,0:T(8,128)S(1)}, f32[2,32,2,8,896]{4,3,2,1,0:T(8,128)S(1)}, f32[25...) custom-call(s32[1,32]{1,0:T(1,128)} %bitcast.10, ...), custom_call_target="tpu_custom_call" | custom-call | tf_op jit(solution)/shard_map/outer_step/pallas_call | solution.py:439
  30.2 4.3 %finish.1 = (f32[2,256,1792]{2,1,0:T(8,128)}, f32[2,256,1792]{2,1,0:T(8,128)}, f32[32,8,1792]{2,1,0:T(8,128)}) custom-call(f32[2,2,4,4,8,1792]{5,4,3,2,1,0:T(8,128)S(1)} %get-tuple-element.10.w, f32[2,2,4,4,8,1792]{5,4,3,2,1,0:T(8,128)S(1)} %get-tuple-element.11.m, f32[2,32,2,8,896]{4,3,2,1,0:T(8,128)S(1)} %get-tuple-element.12.r, ...), custom_call_target="tpu_custom_call" | custom-call | tf_op jit(solution)/shard_map/finish/pallas_call | solution.py:477

commit v5 on v4

--- a/solution.py
+++ b/solution.py
@@ -152,17 +152,12 @@
     q_rows(0)
     q_rows(1)
     pl.semaphore_wait(barrier, len(targets))
-    for copy in side + onward[:2] + direct[:2]:
+    for copy in side + onward[:2]:
         copy.start()
     q_rows(2)
-    for copy in (onward[2], direct[2]):
-        copy.start()
+    onward[2].start()
     q_rows(3)
-    for copy in (onward[3], direct[3]):
-        copy.start()
-    for copy in onward[4:10]:
-        copy.start()
-    for copy in onward[10:14]:
+    for copy in onward[3:14]:
         copy.start()
     own_copy.start()
     own_swap.start()
@@ -227,7 +222,7 @@
     def basis_terms(cols):
         return [terms[:, k * RANK:(k + 1) * RANK, cols].reshape(256, TILE) for k in range(2)]
 
-    for copy in onward[14:] + direct[4:FIRST]:
+    for copy in onward[14:] + direct[:FIRST]:
         copy.start()
     copies[9].wait()
     every = jnp.zeros((256, 256), F32)

time: 34.5 us -> 34.1 us (0.988)
  Pallas kernels: 33.8 us -> 33.3 us
    pallas_call x1, Pallas kernels: 29.5 us -> 29.1 us  [local(): pl.pallas_call(exchange, out_shape=(pltpu.VMEM((2, 2, 4, 4, 8, D), F32),...]
where the time goes in v5:
time: 34.1 us; the launch traced here: 34 us
  Pallas kernels  33.3 us (98%)
  between operations  0.64 us (2%)
    pallas_call x1, Pallas kernels, local(): pl.pallas_call(exchange, out_shape=(pltpu.VMEM((2, 2, 4, 4, 8, D), F32),...  29.1 us
    pallas_call x1, Pallas kernels, local(): pl.pallas_call(finish, out_shape=tuple((jax.ShapeDtypeStruct(shape, F32)...  4.26 us

profile of v5, /device:TPU:1, one launch (start us, length us, event | category | flops | bytes accessed | tf_op | source)
XLA Modules:
  0.0 34.0 jit_solution(3599051473033307688)
XLA Ops:
  0.6 29.1 %outer_step.1 = (f32[2,2,4,4,8,1792]{5,4,3,2,1,0:T(8,128)S(1)}, f32[2,2,4,4,8,1792]{5,4,3,2,1,0:T(8,128)S(1)}, f32[2,32,2,8,896]{4,3,2,1,0:T(8,128)S(1)}, f32[25...) custom-call(s32[1,32]{1,0:T(1,128)} %bitcast.10, ...), custom_call_target="tpu_custom_call" | custom-call | tf_op jit(solution)/shard_map/outer_step/pallas_call | solution.py:434
  29.7 4.3 %finish.1 = (f32[2,256,1792]{2,1,0:T(8,128)}, f32[2,256,1792]{2,1,0:T(8,128)}, f32[32,8,1792]{2,1,0:T(8,128)}) custom-call(f32[2,2,4,4,8,1792]{5,4,3,2,1,0:T(8,128)S(1)} %get-tuple-element.10.w, f32[2,2,4,4,8,1792]{5,4,3,2,1,0:T(8,128)S(1)} %get-tuple-element.11.m, f32[2,32,2,8,896]{4,3,2,1,0:T(8,128)S(1)} %get-tuple-element.12.r, ...), custom_call_target="tpu_custom_call" | custom-call | tf_op jit(solution)/shard_map/finish/pallas_call | solution.py:472

commit v6 on v5

--- a/solution.py
+++ b/solution.py
@@ -27,6 +27,7 @@
        (2, 2), (1, 2), (3, 2), (2, 1), (2, 3),
        (1, 1), (3, 3), (3, 1), (1, 3), (2, 0), (0, 2)]
 FIRST = 9
+GROUP_AT = (7, 9, 11, 12)
 PASSES = [("swap", i) for i in range(4)] + [("side", 15)] + [("side", i) for i in range(4)]
 PASSES += [("side", i) for i in range(4, 8)]
 PASSES += [("swap", i) for i in range(4, 9)] + [("side", i) for i in range(8, 12)]
@@ -377,6 +378,19 @@
         for copy in copies[2 * k:2 * k + 2]:
             copy.start()
 
+    def out_body(b, carry):
+        slot = table[0, b]
+        for half in range(2):
+            cols = slice(half * HALF, (half + 1) * HALF)
+            rows[b, :, cols] = r[half, slot // 2, slot % 2] - (
+                outer_rate * (1.0 + momentum_decay)
+            ) * og[pl.ds(pl.multiple_of(b * 8, 8), 8), cols]
+        return carry
+
+    row_copies = [
+        pltpu.make_async_copy(rows.at[pl.ds(g * 8, 8)], replica.at[pl.ds(g * 8, 8)], row_sem.at[g])
+        for g in range(4)
+    ]
     for j in range(2):
         layer = jnp.sum(jnp.where(lane == 32 + j, table_v[...], 0))
         use = jnp.where(lane == 34 + j, table_v[...], 0)
@@ -397,27 +411,15 @@
                 moved_w.at[j, :, cols], new_weights.at[j, :, cols], sem.at[1, k]))
             if k > 0:
                 issue(k - 1)
-
-    def out_body(b, carry):
-        slot = table[0, b]
-        for half in range(2):
-            cols = slice(half * HALF, (half + 1) * HALF)
-            rows[b, :, cols] = r[half, slot // 2, slot % 2] - (
-                outer_rate * (1.0 + momentum_decay)
-            ) * og[pl.ds(pl.multiple_of(b * 8, 8), 8), cols]
-        return carry
-
-    row_copies = [
-        pltpu.make_async_copy(rows.at[pl.ds(g * 8, 8)], replica.at[pl.ds(g * 8, 8)], row_sem.at[g])
-        for g in range(4)
-    ]
-    table_copy.wait()
-    for g in range(4):
-        lax.fori_loop(g * 8, g * 8 + 8, out_body, 0)
-        if g == 0:
-            issue(2 * (D // TILE) - 1)
-        else:
-            row_copies[g - 1].start()
+            if k in GROUP_AT:
+                g = GROUP_AT.index(k)
+                if g == 0:
+                    table_copy.wait()
+                else:
+                    row_copies[g - 1].start()
+                lax.fori_loop(g * 8, g * 8 + 8, out_body, 0)
+    issue(2 * (D // TILE) - 1)
+
     row_copies[3].start()
     for copy in copies + row_copies:
         copy.wait()

time: 34.1 us -> 34.1 us (level)
  no operation moved by 1% of the time
where the time goes in v6:
time: 34.1 us; the launch traced here: 34 us
  Pallas kernels  33.3 us (98%)
  between operations  0.64 us (2%)
    pallas_call x1, Pallas kernels, local(): pl.pallas_call(exchange, out_shape=(pltpu.VMEM((2, 2, 4, 4, 8, D), F32),...  29.1 us
    pallas_call x1, Pallas kernels, local(): pl.pallas_call(finish, out_shape=tuple((jax.ShapeDtypeStruct(shape, F32)...  4.25 us

profile of v6, /device:TPU:1, one launch (start us, length us, event | category | flops | bytes accessed | tf_op | source)
XLA Modules:
  0.0 34.0 jit_solution(18217347127806401755)
XLA Ops:
  0.6 29.1 %outer_step.1 = (f32[2,2,4,4,8,1792]{5,4,3,2,1,0:T(8,128)S(1)}, f32[2,2,4,4,8,1792]{5,4,3,2,1,0:T(8,128)S(1)}, f32[2,32,2,8,896]{4,3,2,1,0:T(8,128)S(1)}, f32[25...) custom-call(s32[1,32]{1,0:T(1,128)} %bitcast.10, ...), custom_call_target="tpu_custom_call" | custom-call | tf_op jit(solution)/shard_map/outer_step/pallas_call | solution.py:436
  29.7 4.3 %finish.1 = (f32[2,256,1792]{2,1,0:T(8,128)}, f32[2,256,1792]{2,1,0:T(8,128)}, f32[32,8,1792]{2,1,0:T(8,128)}) custom-call(f32[2,2,4,4,8,1792]{5,4,3,2,1,0:T(8,128)S(1)} %get-tuple-element.10.w, f32[2,2,4,4,8,1792]{5,4,3,2,1,0:T(8,128)S(1)} %get-tuple-element.11.m, f32[2,32,2,8,896]{4,3,2,1,0:T(8,128)S(1)} %get-tuple-element.12.r, ...), custom_call_target="tpu_custom_call" | custom-call | tf_op jit(solution)/shard_map/finish/pallas_call | solution.py:474

commit v7 on v6

--- a/solution.py
+++ b/solution.py
@@ -9,7 +9,6 @@
 outer_rate = 0.7
 
 MESH = pl.DeviceIdType.MESH
-HIGHEST = lax.Precision.HIGHEST
 D = 1792
 HALF = D // 2
 RANK = 64
@@ -243,7 +242,8 @@
     slot_lane = jnp.sum(jnp.where(lane256 // 8 == blk_col, slot_col, 0), axis=0, keepdims=True)
     same_row = (row % 8) == (lane256 % 8)
     pick = [
-        jnp.where(((row // 8) * 2 + j == slot_lane) & same_row, 1.0, 0.0) for j in range(2)
+        jnp.where(((row // 8) * 2 + j == slot_lane) & same_row, 1.0, 0.0).astype(BF16)
+        for j in range(2)
     ]
 
     part_copies = [
@@ -262,15 +262,12 @@
     dup = jnp.concatenate(
         [jnp.where(low, averaged, turned), jnp.where(low, turned, averaged)], axis=0
     )
-    chosen = [
-        jnp.dot(p, dup, precision=HIGHEST, preferred_element_type=F32) for p in pick
-    ]
+    dup_high, dup_low = split(dup)
+    chosen = [dot(p, dup_high) + dot(p, dup_low) for p in pick]
     packed[...] = jnp.where(low, chosen[0], chosen[1]).reshape(OWN, 8, 128)
 
     def spread(pairs, keep):
         return jnp.where(keep, jnp.concatenate([pairs, pairs], axis=1), 0.0)
-
-    og_high, og_low = split(spread(dup, in_layer))
 
     takes = core == (lo + y + z + 1) % 2
 
@@ -302,6 +299,8 @@
 
     for i in range(9, 15):
         onward_step(i)
+
+    og_high, og_low = split(spread(dup, in_layer))
 
     def og_body(t, carry):
         cols = pl.ds(pl.multiple_of(t * TILE, TILE), TILE)

time: 34.1 us -> 34.1 us (level)
  no operation moved by 1% of the time
where the time goes in v7:
time: 34.1 us; the launch traced here: 34 us
  Pallas kernels  33.4 us (98%)
  between operations  0.64 us (2%)
    pallas_call x1, Pallas kernels, local(): pl.pallas_call(exchange, out_shape=(pltpu.VMEM((2, 2, 4, 4, 8, D), F32),...  29.1 us
    pallas_call x1, Pallas kernels, local(): pl.pallas_call(finish, out_shape=tuple((jax.ShapeDtypeStruct(shape, F32)...  4.25 us

profile of v7, /device:TPU:1, one launch (start us, length us, event | category | flops | bytes accessed | tf_op | source)
XLA Modules:
  0.0 34.0 jit_solution(17839736539504833023)
XLA Ops:
  0.6 29.1 %outer_step.1 = (f32[2,2,4,4,8,1792]{5,4,3,2,1,0:T(8,128)S(1)}, f32[2,2,4,4,8,1792]{5,4,3,2,1,0:T(8,128)S(1)}, f32[2,32,2,8,896]{4,3,2,1,0:T(8,128)S(1)}, f32[25...) custom-call(s32[1,32]{1,0:T(1,128)} %bitcast.10, ...), custom_call_target="tpu_custom_call" | custom-call | tf_op jit(solution)/shard_map/outer_step/pallas_call | solution.py:435
  29.7 4.3 %finish.1 = (f32[2,256,1792]{2,1,0:T(8,128)}, f32[2,256,1792]{2,1,0:T(8,128)}, f32[32,8,1792]{2,1,0:T(8,128)}) custom-call(f32[2,2,4,4,8,1792]{5,4,3,2,1,0:T(8,128)S(1)} %get-tuple-element.10.w, f32[2,2,4,4,8,1792]{5,4,3,2,1,0:T(8,128)S(1)} %get-tuple-element.11.m, f32[2,32,2,8,896]{4,3,2,1,0:T(8,128)S(1)} %get-tuple-element.12.r, ...), custom_call_target="tpu_custom_call" | custom-call | tf_op jit(solution)/shard_map/finish/pallas_call | solution.py:473
